TPU v7x, 1024 devices: a whole 4x4x32 slice. The times are simulated.
1024 devices in a mesh: ctx: 256 (over z, y, core), head: 4 (over x).
Axes of the slice: x: 4, y: 4, z: 32, core: 2. Of those that a mesh axis runs over, the one named last changes fastest.
Arguments:
- query_raw: bfloat16 [32768, 4096], P('ctx', 'head'), may hold values from -6 to 6
- key_raw: bfloat16 [32768, 512], P('ctx', 'head'), may hold values from -6 to 6
- value_in: bfloat16 [32768, 512], P('ctx', 'head'), may hold values from -6 to 6
- grad_out: bfloat16 [32768, 4096], P('ctx', 'head'), may hold values from -16 to 16
- query_gain: float32 [128], replicated, may hold values from 0.25 to 1.75
- key_gain: float32 [128], replicated, may hold values from 0.25 to 1.75
- loss_table: float32 [16], replicated, may hold values from 0.5 to 8
- loss_bucket: int32 [32768], P('ctx'), may hold values from 0 to 15
- block_docs: int32 [256], P('ctx'), may hold values from 0 to 63, never falling along the last dimension, each value on 1 to 11 neighbouring positions
- query_weight: bfloat16 [4096, 4096], P(None, 'head'), may hold values from -0.09375 to 0.09375
Outputs:
- grad_input: bfloat16 [32768, 4096], P('ctx', 'head')
- grad_key: bfloat16 [32768, 512], P('ctx', 'head')
- grad_value: bfloat16 [32768, 512], P('ctx', 'head')
Inputs may be any that keep to these rules, and one draw needn't show every extreme that they name: `block_docs`: document ids never decrease along the sequence; every document covers 1 to 11 consecutive blocks, and some document covers exactly 11.
All inputs are finite; a program needn't handle non-finite values.
Results may differ from a plain program's by a relative error of at most 0.012.
Values may be sent and summed in bfloat16 or wider, within the bound.
A program may use at most 32 MiB of HBM per device.

v0:
```python
import jax
import jax.numpy as jnp
from jax import lax
from jax.sharding import PartitionSpec as P

QH = 32
KVH = 4
HD = 128
BLOCK = 128
HOPS = 10
NBUCKET = 16


norm_eps = 1e-06


def passed_along(array, axis, by):
    size = lax.axis_size(axis)
    pairs = [(i, i + by) for i in range(size) if 0 <= i + by < size]
    return lax.ppermute(array, axis, pairs)


def from_behind(block, axis, distance):
    devices = range(lax.axis_size(axis))
    route = [((i - distance) % len(devices), i) for i in devices]
    return lax.ppermute(block, axis, route)


def rms_apply(values, gain):
    mean_square = jnp.mean(values * values, axis=-1, keepdims=True)
    return values * lax.rsqrt(mean_square + norm_eps) * gain


def rms_back(values, gain, cotangent):
    result, pullback = jax.vjp(lambda inner: rms_apply(inner, gain), values)
    return pullback(cotangent)[0]


def spread_docs(docs):
    return jnp.broadcast_to(docs[:, None], (docs.shape[0], BLOCK)).reshape(-1)


def local(
    query_raw,
    key_raw,
    value_in,
    grad_out,
    query_gain,
    key_gain,
    loss_table,
    loss_bucket,
    block_docs,
    query_weight,
):
    tokens = query_raw.shape[0]
    kv_local = key_raw.shape[1] // HD
    group = QH // KVH
    scale = HD ** (-0.5)
    rank = lax.axis_index("ctx")
    q_float = query_raw.astype(jnp.float32).reshape(tokens, kv_local, group, HD)
    q_hat = rms_apply(q_float, query_gain).astype(jnp.bfloat16)
    k_float = key_raw.astype(jnp.float32).reshape(tokens, kv_local, HD)
    k_hat = rms_apply(k_float, key_gain).astype(jnp.bfloat16)
    values = value_in.reshape(tokens, kv_local, HD)
    grad_rows = grad_out.reshape(tokens, kv_local, group, HD)
    picks = loss_bucket[:, None] == jnp.arange(NBUCKET, dtype=jnp.int32)[None, :]
    tok_weight = jnp.sum(jnp.where(picks, loss_table[None, :], 0.0), axis=1)
    offsets = jnp.arange(tokens, dtype=jnp.int32)
    q_pos = rank * tokens + offsets
    q_docs = spread_docs(block_docs)

    def block_scores(block, step):
        keys, block_values, docs = block
        source = rank - step
        k_pos = source * tokens + offsets
        allowed = (
            (q_docs[:, None] == spread_docs(docs)[None, :])
            & (k_pos[None, :] <= q_pos[:, None])
            & (source >= 0)
        )
        scores = (
            jnp.einsum("tkgd,skd->kgts", q_hat, keys, preferred_element_type=jnp.float32) * scale
        )
        return jnp.where(allowed[None, None], jnp.exp(scores), 0.0)

    def add_stats(block, step, total, weighted):
        exponent = block_scores(block, step)
        total = total + jnp.sum(exponent, axis=-1)
        weighted = weighted + jnp.einsum(
            "kgts,skd->tkgd",
            exponent.astype(jnp.bfloat16),
            block[1],
            preferred_element_type=jnp.float32,
        )
        return (total, weighted)

    def forward_step(carry, step):
        block, total, weighted = carry
        total, weighted = add_stats(block, step, total, weighted)
        moved = passed_along((block[0], block[1], block[2]), "ctx", 1)
        return ((moved, total, weighted), block)

    start_block = (k_hat, values, block_docs)
    zero_total = jnp.zeros((kv_local, group, tokens), jnp.float32)
    zero_weighted = jnp.zeros((tokens, kv_local, group, HD), jnp.float32)
    (last_block, total, weighted), stash = lax.scan(
        forward_step, (start_block, zero_total, zero_weighted), jnp.arange(HOPS, dtype=jnp.int32)
    )
    total, weighted = add_stats(last_block, HOPS, total, weighted)
    stash = tuple(
        (
            jnp.concatenate([earlier, final[None]], axis=0)
            for earlier, final in zip(stash, last_block)
        )
    )
    attn_out = weighted / jnp.transpose(total, (2, 0, 1))[..., None]
    delta = tok_weight[:, None, None] * jnp.sum(grad_rows.astype(jnp.float32) * attn_out, axis=-1)
    delta_kgt = jnp.transpose(delta, (1, 2, 0))
    weight_row = tok_weight[None, None, :, None]

    def block_grads(block, step):
        keys, block_values, docs = block
        exponent = block_scores(block, step)
        attention = exponent / total[..., None]
        value_dots = jnp.einsum(
            "tkgd,skd->kgts", grad_rows, block_values, preferred_element_type=jnp.float32
        )
        score_grad = attention * (weight_row * value_dots - delta_kgt[..., None])
        ds_half = score_grad.astype(jnp.bfloat16)
        pw_half = (attention * weight_row).astype(jnp.bfloat16)
        dv_part = jnp.einsum(
            "kgts,tkgd->skd", pw_half, grad_rows, preferred_element_type=jnp.float32
        )
        dk_part = (
            jnp.einsum("kgts,tkgd->skd", ds_half, q_hat, preferred_element_type=jnp.float32) * scale
        )
        dq_part = (
            jnp.einsum("kgts,skd->tkgd", ds_half, keys, preferred_element_type=jnp.float32) * scale
        )
        return ((dk_part, dv_part), dq_part)

    zero_kv = jnp.zeros((tokens, kv_local, HD), jnp.float32)

    def relay_step(carry, step):
        grads, dq_sum = carry
        block = tuple((member[step] for member in stash))
        pieces, dq_part = block_grads(block, step)
        grads = (grads[0] + pieces[0], grads[1] + pieces[1])
        moved = from_behind((grads[0], grads[1]), "ctx", 1)
        return ((moved, dq_sum + dq_part), None)

    (grads, dq_sum), unused = lax.scan(
        relay_step, ((zero_kv, zero_kv), zero_weighted), jnp.arange(HOPS, dtype=jnp.int32)
    )
    pieces, dq_part = block_grads(tuple((member[HOPS] for member in stash)), HOPS)
    dq_sum = dq_sum + dq_part
    grads = (grads[0] + pieces[0], grads[1] + pieces[1])
    dk_hat, dv_sum = (
        from_behind(grads[0].astype(jnp.bfloat16), "ctx", -HOPS).astype(jnp.float32),
        from_behind(grads[1].astype(jnp.bfloat16), "ctx", -HOPS).astype(jnp.float32),
    )
    dq_raw = (
        rms_back(q_float, query_gain, dq_sum)
        .astype(jnp.bfloat16)
        .reshape(tokens, kv_local * group * HD)
    )
    term = lax.dot_general(
        dq_raw, query_weight, (((1,), (1,)), ((), ())), preferred_element_type=jnp.float32
    )
    grad_input = lax.psum_scatter(
        term.astype(jnp.bfloat16), "head", scatter_dimension=1, tiled=True
    )
    grad_key = (
        rms_back(k_float, key_gain, dk_hat).astype(jnp.bfloat16).reshape(tokens, kv_local * HD)
    )
    grad_value = dv_sum.astype(jnp.bfloat16).reshape(tokens, kv_local * HD)
    return (grad_input, grad_key, grad_value)


def solution(mesh):
    placed = (
        P("ctx", "head"),
        P("ctx", "head"),
        P("ctx", "head"),
        P("ctx", "head"),
        P(),
        P(),
        P(),
        P("ctx"),
        P("ctx"),
        P(None, "head"),
    )
    return jax.shard_map(
        local,
        mesh=mesh,
        in_specs=placed,
        out_specs=(P("ctx", "head"), P("ctx", "head"), P("ctx", "head")),
        check_vma=False,
    )
```

profile of v0, /device:TPU:24, one launch (start us, length us, event | category | flops | bytes accessed | tf_op | source)
XLA Modules:
  0.0 392.2 jit_solution(3359582725369189954)
XLA Ops:
  14.9 144.1 %while.40 = (s32[]{:T(128)}, bf16[128,1,128]{2,0,1:T(8,128)(2,1)S(1)}, bf16[128,1,128]{2,0,1:T(8,128)(2,1)S(1)}, s32[1]{0:T(128)}, f32[1,8,128]{2,1,0:T(8,128)S(...) while((s32[]{:T(128)}, ...), condition=%wide.region_4.5_spmd.clone, body=%wide.region_2.0_spmd.clone.sunk | while | flops 67945728 | bytes 2476432 | solution.py:106
  14.9 1.9 collective-permute-start
  16.8 3.6 collective-permute-start.1
  20.4 2.7 collective-permute-start.2
  28.4 3.5 collective-permute-start
  31.9 2.0 collective-permute-start.1
  33.9 4.3 %collective-permute-start.2 = (s32[1]{0:T(128)}, s32[1]{0:T(128)}, u32[]{:S(2)}, u32[]{:S(2)}) collective-permute-start(s32[1]{0:T(128)} %copy.103), channel_id=1, source_target_pairs={{0,4},{4,8},{8,12},{12,16},{16,20},{20,24},{24,28},{28,32},{32,36}... | collective-permute-start | bytes 20 | tf_op jit(solution)/shard_map/while/body/eval_jaxpr/ppermute | solution.py:20
  41.5 1.4 dynamic_update_slice.19
  43.6 1.9 collective-permute-start
  45.5 3.3 collective-permute-start.1
  48.8 2.7 collective-permute-start.2
  54.8 1.4 dynamic_update_slice.19
  56.9 3.5 collective-permute-start
  60.4 2.0 collective-permute-start.1
  62.4 4.3 %collective-permute-start.2 = (s32[1]{0:T(128)}, s32[1]{0:T(128)}, u32[]{:S(2)}, u32[]{:S(2)}) collective-permute-start(s32[1]{0:T(128)} %copy.103), channel_id=1, source_target_pairs={{0,4},{4,8},{8,12},{12,16},{16,20},{20,24},{24,28},{28,32},{32,36}... | collective-permute-start | bytes 20 | tf_op jit(solution)/shard_map/while/body/eval_jaxpr/ppermute | solution.py:20
  69.9 1.4 dynamic_update_slice.19
  72.0 1.9 collective-permute-start
  74.0 3.6 collective-permute-start.1
  77.6 2.7 collective-permute-start.2
  83.5 1.4 dynamic_update_slice.19
  85.6 3.2 collective-permute-start
  88.8 2.0 collective-permute-start.1
  90.9 4.3 %collective-permute-start.2 = (s32[1]{0:T(128)}, s32[1]{0:T(128)}, u32[]{:S(2)}, u32[]{:S(2)}) collective-permute-start(s32[1]{0:T(128)} %copy.103), channel_id=1, source_target_pairs={{0,4},{4,8},{8,12},{12,16},{16,20},{20,24},{24,28},{28,32},{32,36}... | collective-permute-start | bytes 20 | tf_op jit(solution)/shard_map/while/body/eval_jaxpr/ppermute | solution.py:20
  100.5 1.9 collective-permute-start
  102.5 3.6 collective-permute-start.1
  106.0 2.8 collective-permute-start.2
  112.0 1.4 dynamic_update_slice.19
  114.1 3.5 collective-permute-start
  117.6 2.0 collective-permute-start.1
  119.6 4.0 %collective-permute-start.2 = (s32[1]{0:T(128)}, s32[1]{0:T(128)}, u32[]{:S(2)}, u32[]{:S(2)}) collective-permute-start(s32[1]{0:T(128)} %copy.103), channel_id=1, source_target_pairs={{0,4},{4,8},{8,12},{12,16},{16,20},{20,24},{24,28},{28,32},{32,36}... | collective-permute-start | bytes 20 | tf_op jit(solution)/shard_map/while/body/eval_jaxpr/ppermute | solution.py:20
  129.0 1.9 collective-permute-start
  130.9 4.8 %collective-permute-start.1 = (bf16[128,1,128]{2,0,1:T(8,128)(2,1)S(1)}, bf16[128,1,128]{2,0,1:T(8,128)(2,1)S(1)}, u32[]{:S(2)}, u32[]{:S(2)}) collective-permute-start(bf16[128,1,128]{2,0,1:T(8,128)(2,1)S(1)} %copy.102), channel_id=1, source_target_pairs={{0,4},{4,8},{8,12},{12,16},{16,20},{20,24},{24,28},{28,32},{32,36}... | collective-permute-start | bytes 98312 | tf_op jit(solution)/shard_map/while/body/eval_jaxpr/ppermute | solution.py:20
  135.7 2.7 collective-permute-start.2
  143.8 3.5 collective-permute-start
  147.3 2.9 collective-permute-start.1
  150.2 3.4 collective-permute-start.2
  161.2 1.4 fusion.67
  165.0 154.2 %while.41 = (s32[]{:T(128)}, f32[128,1,128]{2,0,1:T(8,128)S(1)}, f32[128,1,128]{2,0,1:T(8,128)S(1)}, f32[128,1,8,128]{0,3,2,1:T(8,128)S(1)}, s32[10]{0:T(128)S(1...) while((s32[]{:T(128)}, f32[128,1,128]{2,0,1:T(8,128)S(1)}, ...), condition=%wide.region_9.10_spmd.clone, body=%wide.region_8.9_spmd.clone.sunk | while | flops 169443584 | bytes 5385609 | solution.py:152
  170.9 1.9 collective-permute-start.3
  173.1 3.3 collective-permute-start.4
  176.7 1.9 collective-permute-done.4
  184.6 1.9 collective-permute-start.3
  186.7 5.4 %collective-permute-start.4 = (f32[128,1,128]{2,0,1:T(8,128)S(1)}, f32[128,1,128]{2,0,1:T(8,128)S(1)}, u32[]{:S(2)}, u32[]{:S(2)}) collective-permute-start(f32[128,1,128]{2,0,1:T(8,128)S(1)} %fusion.155), channel_id=1, source_target_pairs={{1020,0},{0,4},{4,8},{8,12},{12,16},{16,20},{20,24},{24,28},{28,32... | collective-permute-start | bytes 196616 | tf_op jit(solution)/shard_map/while/body/eval_jaxpr/ppermute | solution.py:26
  198.9 2.4 collective-permute-start.3
  201.5 6.4 %collective-permute-start.4 = (f32[128,1,128]{2,0,1:T(8,128)S(1)}, f32[128,1,128]{2,0,1:T(8,128)S(1)}, u32[]{:S(2)}, u32[]{:S(2)}) collective-permute-start(f32[128,1,128]{2,0,1:T(8,128)S(1)} %fusion.155), channel_id=1, source_target_pairs={{1020,0},{0,4},{4,8},{8,12},{12,16},{16,20},{20,24},{24,28},{28,32... | collective-permute-start | bytes 196616 | tf_op jit(solution)/shard_map/while/body/eval_jaxpr/ppermute | solution.py:26
  214.7 2.4 collective-permute-start.3
  217.3 6.4 %collective-permute-start.4 = (f32[128,1,128]{2,0,1:T(8,128)S(1)}, f32[128,1,128]{2,0,1:T(8,128)S(1)}, u32[]{:S(2)}, u32[]{:S(2)}) collective-permute-start(f32[128,1,128]{2,0,1:T(8,128)S(1)} %fusion.155), channel_id=1, source_target_pairs={{1020,0},{0,4},{4,8},{8,12},{12,16},{16,20},{20,24},{24,28},{28,32... | collective-permute-start | bytes 196616 | tf_op jit(solution)/shard_map/while/body/eval_jaxpr/ppermute | solution.py:26
  230.5 2.4 collective-permute-start.3
  233.1 6.4 %collective-permute-start.4 = (f32[128,1,128]{2,0,1:T(8,128)S(1)}, f32[128,1,128]{2,0,1:T(8,128)S(1)}, u32[]{:S(2)}, u32[]{:S(2)}) collective-permute-start(f32[128,1,128]{2,0,1:T(8,128)S(1)} %fusion.155), channel_id=1, source_target_pairs={{1020,0},{0,4},{4,8},{8,12},{12,16},{16,20},{20,24},{24,28},{28,32... | collective-permute-start | bytes 196616 | tf_op jit(solution)/shard_map/while/body/eval_jaxpr/ppermute | solution.py:26
  246.3 2.4 collective-permute-start.3
  248.9 6.4 %collective-permute-start.4 = (f32[128,1,128]{2,0,1:T(8,128)S(1)}, f32[128,1,128]{2,0,1:T(8,128)S(1)}, u32[]{:S(2)}, u32[]{:S(2)}) collective-permute-start(f32[128,1,128]{2,0,1:T(8,128)S(1)} %fusion.155), channel_id=1, source_target_pairs={{1020,0},{0,4},{4,8},{8,12},{12,16},{16,20},{20,24},{24,28},{28,32... | collective-permute-start | bytes 196616 | tf_op jit(solution)/shard_map/while/body/eval_jaxpr/ppermute | solution.py:26
  262.0 2.4 collective-permute-start.3
  264.6 6.4 %collective-permute-start.4 = (f32[128,1,128]{2,0,1:T(8,128)S(1)}, f32[128,1,128]{2,0,1:T(8,128)S(1)}, u32[]{:S(2)}, u32[]{:S(2)}) collective-permute-start(f32[128,1,128]{2,0,1:T(8,128)S(1)} %fusion.155), channel_id=1, source_target_pairs={{1020,0},{0,4},{4,8},{8,12},{12,16},{16,20},{20,24},{24,28},{28,32... | collective-permute-start | bytes 196616 | tf_op jit(solution)/shard_map/while/body/eval_jaxpr/ppermute | solution.py:26
  277.8 2.4 collective-permute-start.3
  280.4 6.4 %collective-permute-start.4 = (f32[128,1,128]{2,0,1:T(8,128)S(1)}, f32[128,1,128]{2,0,1:T(8,128)S(1)}, u32[]{:S(2)}, u32[]{:S(2)}) collective-permute-start(f32[128,1,128]{2,0,1:T(8,128)S(1)} %fusion.155), channel_id=1, source_target_pairs={{1020,0},{0,4},{4,8},{8,12},{12,16},{16,20},{20,24},{24,28},{28,32... | collective-permute-start | bytes 196616 | tf_op jit(solution)/shard_map/while/body/eval_jaxpr/ppermute | solution.py:26
  293.6 2.4 collective-permute-start.3
  296.2 6.4 %collective-permute-start.4 = (f32[128,1,128]{2,0,1:T(8,128)S(1)}, f32[128,1,128]{2,0,1:T(8,128)S(1)}, u32[]{:S(2)}, u32[]{:S(2)}) collective-permute-start(f32[128,1,128]{2,0,1:T(8,128)S(1)} %fusion.155), channel_id=1, source_target_pairs={{1020,0},{0,4},{4,8},{8,12},{12,16},{16,20},{20,24},{24,28},{28,32... | collective-permute-start | bytes 196616 | tf_op jit(solution)/shard_map/while/body/eval_jaxpr/ppermute | solution.py:26
  309.3 2.4 collective-permute-start.3
  311.9 6.4 %collective-permute-start.4 = (f32[128,1,128]{2,0,1:T(8,128)S(1)}, f32[128,1,128]{2,0,1:T(8,128)S(1)}, u32[]{:S(2)}, u32[]{:S(2)}) collective-permute-start(f32[128,1,128]{2,0,1:T(8,128)S(1)} %fusion.155), channel_id=1, source_target_pairs={{1020,0},{0,4},{4,8},{8,12},{12,16},{16,20},{20,24},{24,28},{28,32... | collective-permute-start | bytes 196616 | tf_op jit(solution)/shard_map/while/body/eval_jaxpr/ppermute | solution.py:26
  319.7 7.2 %convolution_convert_fusion = bf16[128,4096]{1,0:T(8,128)(2,1)} fusion(bf16[128,1024]{0,1:T(8,128)(2,1)S(1)} %bitcast.397, bf16[4096,1024]{1,0:T(8,128)(2,1)} %param.23), kind=kOutput, calls=%fused_computation.64 | convolution fusion | flops 1074266112 | bytes 9699328 | tf_op jit(solution)/shard_map/dot_general | solution.py:167
  327.3 8.4 %collective-permute-start.5 = (bf16[128,1,128]{0,2,1:T(8,128)(2,1)S(1)}, bf16[128,1,128]{0,2,1:T(8,128)(2,1)S(1)}, u32[]{:S(2)}, u32[]{:S(2)}) collective-permute-start(bf16[128,1,128]{0,2,1:T(8,128)(2,1)S(1)} %fusion.73), channel_id=1, source_target_pairs={{40,0},{44,4},{48,8},{52,12},{56,16},{60,20},{64,24},{68,28},{72,3... | collective-permute-start | bytes 98312 | tf_op jit(solution)/shard_map/ppermute | solution.py:26
  336.0 1.9 collective-permute-start.6
  339.1 5.7 %collective-permute-done.6 = bf16[128,1,128]{2,0,1:T(8,128)(2,1)S(1)} collective-permute-done((bf16[128,1,128]{2,0,1:T(8,128)(2,1)S(1)}, bf16[128,1,128]{2,0,1:T(8,128)(2,1)S(1)}, u32[]{:S(2)}, u32[]{:S(2)}) %collective-permute-start.6) | collective-permute-done | bytes 32800 | tf_op jit(solution)/shard_map/ppermute | solution.py:26
  344.8 40.0 %reduce-scatter.2.cloned.1.call-done = bf16[128,1024]{1,0:T(8,128)(2,1)} async-done(((bf16[128,4096]{1,0:T(8,128)(2,1)}), bf16[128,1024]{1,0:T(8,128)(2,1)}) %reduce-scatter.2.cloned.1.call-update) | async-done | bytes 262160 | tf_op jit(solution)/shard_map/reduce_scatter | solution.py:170
  (322 shorter events, 70.2 us)
Async XLA Ops:
  7.2 377.6 %reduce-scatter.2.cloned.1.call-start = ((), (), s32[]{:S(2)}) async-start(), calls=%async_computation.1 | async-start | bytes 1310720 | tf_op jit(solution)/shard_map/reduce_scatter | solution.py:170
  13.2 147.5 %copy-start = (bf16[128,1024]{1,0:T(8,128)(2,1)S(1)}, bf16[128,1024]{1,0:T(8,128)(2,1)}, u32[]{:S(2)}) copy-start(bf16[128,1024]{1,0:T(8,128)(2,1)} %param.14) | copy-start | bytes 786436
  13.5 147.6 %copy-start.12 = (f32[16]{0:T(128)S(1)}, f32[16]{0:T(128)}, u32[]{:S(2)}) copy-start(f32[16]{0:T(128)} %param.20) | copy-start | bytes 196
  13.5 147.6 %copy-start.13 = (s32[128]{0:T(128)S(1)}, s32[128]{0:T(128)}, u32[]{:S(2)}) copy-start(s32[128]{0:T(128)} %param.21) | copy-start | bytes 1540
  14.9 12.8 %collective-permute-start = (bf16[128,1,128]{2,0,1:T(8,128)(2,1)S(1)}, bf16[128,1,128]{2,0,1:T(8,128)(2,1)S(1)}, u32[]{:S(2)}, u32[]{:S(2)}) collective-permute-start(bf16[128,1,128]{2,0,1:T(8,128)(2,1)S(1)} %copy.101), channel_id=1, source_target_pairs={{0,4},{4,8},{8,12},{12,16},{16,20},{20,24},{24,28},{28,32},{32,36}... | collective-permute-start | bytes 98312 | tf_op jit(solution)/shard_map/while/body/eval_jaxpr/ppermute | solution.py:20
  16.8 10.8 %collective-permute-start.1 = (bf16[128,1,128]{2,0,1:T(8,128)(2,1)S(1)}, bf16[128,1,128]{2,0,1:T(8,128)(2,1)S(1)}, u32[]{:S(2)}, u32[]{:S(2)}) collective-permute-start(bf16[128,1,128]{2,0,1:T(8,128)(2,1)S(1)} %copy.102), channel_id=1, source_target_pairs={{0,4},{4,8},{8,12},{12,16},{16,20},{20,24},{24,28},{28,32},{32,36}... | collective-permute-start | bytes 98312 | tf_op jit(solution)/shard_map/while/body/eval_jaxpr/ppermute | solution.py:20
  20.4 7.2 %collective-permute-start.2 = (s32[1]{0:T(128)}, s32[1]{0:T(128)}, u32[]{:S(2)}, u32[]{:S(2)}) collective-permute-start(s32[1]{0:T(128)} %copy.103), channel_id=1, source_target_pairs={{0,4},{4,8},{8,12},{12,16},{16,20},{20,24},{24,28},{28,32},{32,36}... | collective-permute-start | bytes 20 | tf_op jit(solution)/shard_map/while/body/eval_jaxpr/ppermute | solution.py:20
  28.4 14.4 %collective-permute-start = (bf16[128,1,128]{2,0,1:T(8,128)(2,1)S(1)}, bf16[128,1,128]{2,0,1:T(8,128)(2,1)S(1)}, u32[]{:S(2)}, u32[]{:S(2)}) collective-permute-start(bf16[128,1,128]{2,0,1:T(8,128)(2,1)S(1)} %copy.101), channel_id=1, source_target_pairs={{0,4},{4,8},{8,12},{12,16},{16,20},{20,24},{24,28},{28,32},{32,36}... | collective-permute-start | bytes 98312 | tf_op jit(solution)/shard_map/while/body/eval_jaxpr/ppermute | solution.py:20
  31.9 10.9 %collective-permute-start.1 = (bf16[128,1,128]{2,0,1:T(8,128)(2,1)S(1)}, bf16[128,1,128]{2,0,1:T(8,128)(2,1)S(1)}, u32[]{:S(2)}, u32[]{:S(2)}) collective-permute-start(bf16[128,1,128]{2,0,1:T(8,128)(2,1)S(1)} %copy.102), channel_id=1, source_target_pairs={{0,4},{4,8},{8,12},{12,16},{16,20},{20,24},{24,28},{28,32},{32,36}... | collective-permute-start | bytes 98312 | tf_op jit(solution)/shard_map/while/body/eval_jaxpr/ppermute | solution.py:20
  33.9 8.9 %collective-permute-start.2 = (s32[1]{0:T(128)}, s32[1]{0:T(128)}, u32[]{:S(2)}, u32[]{:S(2)}) collective-permute-start(s32[1]{0:T(128)} %copy.103), channel_id=1, source_target_pairs={{0,4},{4,8},{8,12},{12,16},{16,20},{20,24},{24,28},{28,32},{32,36}... | collective-permute-start | bytes 20 | tf_op jit(solution)/shard_map/while/body/eval_jaxpr/ppermute | solution.py:20
  43.6 12.6 %collective-permute-start = (bf16[128,1,128]{2,0,1:T(8,128)(2,1)S(1)}, bf16[128,1,128]{2,0,1:T(8,128)(2,1)S(1)}, u32[]{:S(2)}, u32[]{:S(2)}) collective-permute-start(bf16[128,1,128]{2,0,1:T(8,128)(2,1)S(1)} %copy.101), channel_id=1, source_target_pairs={{0,4},{4,8},{8,12},{12,16},{16,20},{20,24},{24,28},{28,32},{32,36}... | collective-permute-start | bytes 98312 | tf_op jit(solution)/shard_map/while/body/eval_jaxpr/ppermute | solution.py:20
  45.5 10.6 %collective-permute-start.1 = (bf16[128,1,128]{2,0,1:T(8,128)(2,1)S(1)}, bf16[128,1,128]{2,0,1:T(8,128)(2,1)S(1)}, u32[]{:S(2)}, u32[]{:S(2)}) collective-permute-start(bf16[128,1,128]{2,0,1:T(8,128)(2,1)S(1)} %copy.102), channel_id=1, source_target_pairs={{0,4},{4,8},{8,12},{12,16},{16,20},{20,24},{24,28},{28,32},{32,36}... | collective-permute-start | bytes 98312 | tf_op jit(solution)/shard_map/while/body/eval_jaxpr/ppermute | solution.py:20
  48.8 7.3 %collective-permute-start.2 = (s32[1]{0:T(128)}, s32[1]{0:T(128)}, u32[]{:S(2)}, u32[]{:S(2)}) collective-permute-start(s32[1]{0:T(128)} %copy.103), channel_id=1, source_target_pairs={{0,4},{4,8},{8,12},{12,16},{16,20},{20,24},{24,28},{28,32},{32,36}... | collective-permute-start | bytes 20 | tf_op jit(solution)/shard_map/while/body/eval_jaxpr/ppermute | solution.py:20
  56.9 14.4 %collective-permute-start = (bf16[128,1,128]{2,0,1:T(8,128)(2,1)S(1)}, bf16[128,1,128]{2,0,1:T(8,128)(2,1)S(1)}, u32[]{:S(2)}, u32[]{:S(2)}) collective-permute-start(bf16[128,1,128]{2,0,1:T(8,128)(2,1)S(1)} %copy.101), channel_id=1, source_target_pairs={{0,4},{4,8},{8,12},{12,16},{16,20},{20,24},{24,28},{28,32},{32,36}... | collective-permute-start | bytes 98312 | tf_op jit(solution)/shard_map/while/body/eval_jaxpr/ppermute | solution.py:20
  60.4 10.9 %collective-permute-start.1 = (bf16[128,1,128]{2,0,1:T(8,128)(2,1)S(1)}, bf16[128,1,128]{2,0,1:T(8,128)(2,1)S(1)}, u32[]{:S(2)}, u32[]{:S(2)}) collective-permute-start(bf16[128,1,128]{2,0,1:T(8,128)(2,1)S(1)} %copy.102), channel_id=1, source_target_pairs={{0,4},{4,8},{8,12},{12,16},{16,20},{20,24},{24,28},{28,32},{32,36}... | collective-permute-start | bytes 98312 | tf_op jit(solution)/shard_map/while/body/eval_jaxpr/ppermute | solution.py:20
  62.4 8.9 %collective-permute-start.2 = (s32[1]{0:T(128)}, s32[1]{0:T(128)}, u32[]{:S(2)}, u32[]{:S(2)}) collective-permute-start(s32[1]{0:T(128)} %copy.103), channel_id=1, source_target_pairs={{0,4},{4,8},{8,12},{12,16},{16,20},{20,24},{24,28},{28,32},{32,36}... | collective-permute-start | bytes 20 | tf_op jit(solution)/shard_map/while/body/eval_jaxpr/ppermute | solution.py:20
  72.0 12.9 %collective-permute-start = (bf16[128,1,128]{2,0,1:T(8,128)(2,1)S(1)}, bf16[128,1,128]{2,0,1:T(8,128)(2,1)S(1)}, u32[]{:S(2)}, u32[]{:S(2)}) collective-permute-start(bf16[128,1,128]{2,0,1:T(8,128)(2,1)S(1)} %copy.101), channel_id=1, source_target_pairs={{0,4},{4,8},{8,12},{12,16},{16,20},{20,24},{24,28},{28,32},{32,36}... | collective-permute-start | bytes 98312 | tf_op jit(solution)/shard_map/while/body/eval_jaxpr/ppermute | solution.py:20
  74.0 10.9 %collective-permute-start.1 = (bf16[128,1,128]{2,0,1:T(8,128)(2,1)S(1)}, bf16[128,1,128]{2,0,1:T(8,128)(2,1)S(1)}, u32[]{:S(2)}, u32[]{:S(2)}) collective-permute-start(bf16[128,1,128]{2,0,1:T(8,128)(2,1)S(1)} %copy.102), channel_id=1, source_target_pairs={{0,4},{4,8},{8,12},{12,16},{16,20},{20,24},{24,28},{28,32},{32,36}... | collective-permute-start | bytes 98312 | tf_op jit(solution)/shard_map/while/body/eval_jaxpr/ppermute | solution.py:20
  77.6 7.3 %collective-permute-start.2 = (s32[1]{0:T(128)}, s32[1]{0:T(128)}, u32[]{:S(2)}, u32[]{:S(2)}) collective-permute-start(s32[1]{0:T(128)} %copy.103), channel_id=1, source_target_pairs={{0,4},{4,8},{8,12},{12,16},{16,20},{20,24},{24,28},{28,32},{32,36}... | collective-permute-start | bytes 20 | tf_op jit(solution)/shard_map/while/body/eval_jaxpr/ppermute | solution.py:20
  85.6 14.1 %collective-permute-start = (bf16[128,1,128]{2,0,1:T(8,128)(2,1)S(1)}, bf16[128,1,128]{2,0,1:T(8,128)(2,1)S(1)}, u32[]{:S(2)}, u32[]{:S(2)}) collective-permute-start(bf16[128,1,128]{2,0,1:T(8,128)(2,1)S(1)} %copy.101), channel_id=1, source_target_pairs={{0,4},{4,8},{8,12},{12,16},{16,20},{20,24},{24,28},{28,32},{32,36}... | collective-permute-start | bytes 98312 | tf_op jit(solution)/shard_map/while/body/eval_jaxpr/ppermute | solution.py:20
  88.8 10.9 %collective-permute-start.1 = (bf16[128,1,128]{2,0,1:T(8,128)(2,1)S(1)}, bf16[128,1,128]{2,0,1:T(8,128)(2,1)S(1)}, u32[]{:S(2)}, u32[]{:S(2)}) collective-permute-start(bf16[128,1,128]{2,0,1:T(8,128)(2,1)S(1)} %copy.102), channel_id=1, source_target_pairs={{0,4},{4,8},{8,12},{12,16},{16,20},{20,24},{24,28},{28,32},{32,36}... | collective-permute-start | bytes 98312 | tf_op jit(solution)/shard_map/while/body/eval_jaxpr/ppermute | solution.py:20
  90.9 8.9 %collective-permute-start.2 = (s32[1]{0:T(128)}, s32[1]{0:T(128)}, u32[]{:S(2)}, u32[]{:S(2)}) collective-permute-start(s32[1]{0:T(128)} %copy.103), channel_id=1, source_target_pairs={{0,4},{4,8},{8,12},{12,16},{16,20},{20,24},{24,28},{28,32},{32,36}... | collective-permute-start | bytes 20 | tf_op jit(solution)/shard_map/while/body/eval_jaxpr/ppermute | solution.py:20
  100.5 12.9 %collective-permute-start = (bf16[128,1,128]{2,0,1:T(8,128)(2,1)S(1)}, bf16[128,1,128]{2,0,1:T(8,128)(2,1)S(1)}, u32[]{:S(2)}, u32[]{:S(2)}) collective-permute-start(bf16[128,1,128]{2,0,1:T(8,128)(2,1)S(1)} %copy.101), channel_id=1, source_target_pairs={{0,4},{4,8},{8,12},{12,16},{16,20},{20,24},{24,28},{28,32},{32,36}... | collective-permute-start | bytes 98312 | tf_op jit(solution)/shard_map/while/body/eval_jaxpr/ppermute | solution.py:20
  102.5 10.9 %collective-permute-start.1 = (bf16[128,1,128]{2,0,1:T(8,128)(2,1)S(1)}, bf16[128,1,128]{2,0,1:T(8,128)(2,1)S(1)}, u32[]{:S(2)}, u32[]{:S(2)}) collective-permute-start(bf16[128,1,128]{2,0,1:T(8,128)(2,1)S(1)} %copy.102), channel_id=1, source_target_pairs={{0,4},{4,8},{8,12},{12,16},{16,20},{20,24},{24,28},{28,32},{32,36}... | collective-permute-start | bytes 98312 | tf_op jit(solution)/shard_map/while/body/eval_jaxpr/ppermute | solution.py:20
  106.0 7.3 %collective-permute-start.2 = (s32[1]{0:T(128)}, s32[1]{0:T(128)}, u32[]{:S(2)}, u32[]{:S(2)}) collective-permute-start(s32[1]{0:T(128)} %copy.103), channel_id=1, source_target_pairs={{0,4},{4,8},{8,12},{12,16},{16,20},{20,24},{24,28},{28,32},{32,36}... | collective-permute-start | bytes 20 | tf_op jit(solution)/shard_map/while/body/eval_jaxpr/ppermute | solution.py:20
  114.1 14.1 %collective-permute-start = (bf16[128,1,128]{2,0,1:T(8,128)(2,1)S(1)}, bf16[128,1,128]{2,0,1:T(8,128)(2,1)S(1)}, u32[]{:S(2)}, u32[]{:S(2)}) collective-permute-start(bf16[128,1,128]{2,0,1:T(8,128)(2,1)S(1)} %copy.101), channel_id=1, source_target_pairs={{0,4},{4,8},{8,12},{12,16},{16,20},{20,24},{24,28},{28,32},{32,36}... | collective-permute-start | bytes 98312 | tf_op jit(solution)/shard_map/while/body/eval_jaxpr/ppermute | solution.py:20
  117.6 10.6 %collective-permute-start.1 = (bf16[128,1,128]{2,0,1:T(8,128)(2,1)S(1)}, bf16[128,1,128]{2,0,1:T(8,128)(2,1)S(1)}, u32[]{:S(2)}, u32[]{:S(2)}) collective-permute-start(bf16[128,1,128]{2,0,1:T(8,128)(2,1)S(1)} %copy.102), channel_id=1, source_target_pairs={{0,4},{4,8},{8,12},{12,16},{16,20},{20,24},{24,28},{28,32},{32,36}... | collective-permute-start | bytes 98312 | tf_op jit(solution)/shard_map/while/body/eval_jaxpr/ppermute | solution.py:20
  119.6 8.6 %collective-permute-start.2 = (s32[1]{0:T(128)}, s32[1]{0:T(128)}, u32[]{:S(2)}, u32[]{:S(2)}) collective-permute-start(s32[1]{0:T(128)} %copy.103), channel_id=1, source_target_pairs={{0,4},{4,8},{8,12},{12,16},{16,20},{20,24},{24,28},{28,32},{32,36}... | collective-permute-start | bytes 20 | tf_op jit(solution)/shard_map/while/body/eval_jaxpr/ppermute | solution.py:20
  129.0 14.1 %collective-permute-start = (bf16[128,1,128]{2,0,1:T(8,128)(2,1)S(1)}, bf16[128,1,128]{2,0,1:T(8,128)(2,1)S(1)}, u32[]{:S(2)}, u32[]{:S(2)}) collective-permute-start(bf16[128,1,128]{2,0,1:T(8,128)(2,1)S(1)} %copy.101), channel_id=1, source_target_pairs={{0,4},{4,8},{8,12},{12,16},{16,20},{20,24},{24,28},{28,32},{32,36}... | collective-permute-start | bytes 98312 | tf_op jit(solution)/shard_map/while/body/eval_jaxpr/ppermute | solution.py:20
  130.9 12.2 %collective-permute-start.1 = (bf16[128,1,128]{2,0,1:T(8,128)(2,1)S(1)}, bf16[128,1,128]{2,0,1:T(8,128)(2,1)S(1)}, u32[]{:S(2)}, u32[]{:S(2)}) collective-permute-start(bf16[128,1,128]{2,0,1:T(8,128)(2,1)S(1)} %copy.102), channel_id=1, source_target_pairs={{0,4},{4,8},{8,12},{12,16},{16,20},{20,24},{24,28},{28,32},{32,36}... | collective-permute-start | bytes 98312 | tf_op jit(solution)/shard_map/while/body/eval_jaxpr/ppermute | solution.py:20
  135.7 7.3 %collective-permute-start.2 = (s32[1]{0:T(128)}, s32[1]{0:T(128)}, u32[]{:S(2)}, u32[]{:S(2)}) collective-permute-start(s32[1]{0:T(128)} %copy.103), channel_id=1, source_target_pairs={{0,4},{4,8},{8,12},{12,16},{16,20},{20,24},{24,28},{28,32},{32,36}... | collective-permute-start | bytes 20 | tf_op jit(solution)/shard_map/while/body/eval_jaxpr/ppermute | solution.py:20
  143.8 14.4 %collective-permute-start = (bf16[128,1,128]{2,0,1:T(8,128)(2,1)S(1)}, bf16[128,1,128]{2,0,1:T(8,128)(2,1)S(1)}, u32[]{:S(2)}, u32[]{:S(2)}) collective-permute-start(bf16[128,1,128]{2,0,1:T(8,128)(2,1)S(1)} %copy.101), channel_id=1, source_target_pairs={{0,4},{4,8},{8,12},{12,16},{16,20},{20,24},{24,28},{28,32},{32,36}... | collective-permute-start | bytes 98312 | tf_op jit(solution)/shard_map/while/body/eval_jaxpr/ppermute | solution.py:20
  147.3 10.9 %collective-permute-start.1 = (bf16[128,1,128]{2,0,1:T(8,128)(2,1)S(1)}, bf16[128,1,128]{2,0,1:T(8,128)(2,1)S(1)}, u32[]{:S(2)}, u32[]{:S(2)}) collective-permute-start(bf16[128,1,128]{2,0,1:T(8,128)(2,1)S(1)} %copy.102), channel_id=1, source_target_pairs={{0,4},{4,8},{8,12},{12,16},{16,20},{20,24},{24,28},{28,32},{32,36}... | collective-permute-start | bytes 98312 | tf_op jit(solution)/shard_map/while/body/eval_jaxpr/ppermute | solution.py:20
  150.2 8.0 %collective-permute-start.2 = (s32[1]{0:T(128)}, s32[1]{0:T(128)}, u32[]{:S(2)}, u32[]{:S(2)}) collective-permute-start(s32[1]{0:T(128)} %copy.103), channel_id=1, source_target_pairs={{0,4},{4,8},{8,12},{12,16},{16,20},{20,24},{24,28},{28,32},{32,36}... | collective-permute-start | bytes 20 | tf_op jit(solution)/shard_map/while/body/eval_jaxpr/ppermute | solution.py:20
  161.0 3.9 copy-start.3
  165.0 154.3 %copy-start.6 = (f32[128]{0:T(128)S(1)}, f32[128]{0:T(128)}, u32[]{:S(2)}) copy-start(f32[128]{0:T(128)} %param.18) | copy-start | bytes 1540
  170.9 5.8 %collective-permute-start.3 = (f32[128,1,128]{2,0,1:T(8,128)S(1)}, f32[128,1,128]{2,0,1:T(8,128)S(1)}, u32[]{:S(2)}, u32[]{:S(2)}) collective-permute-start(f32[128,1,128]{2,0,1:T(8,128)S(1)} %fusion.154), channel_id=1, source_target_pairs={{1020,0},{0,4},{4,8},{8,12},{12,16},{16,20},{20,24},{24,28},{28,32... | collective-permute-start | bytes 196616 | tf_op jit(solution)/shard_map/while/body/eval_jaxpr/ppermute | solution.py:26
  173.1 5.6 %collective-permute-start.4 = (f32[128,1,128]{2,0,1:T(8,128)S(1)}, f32[128,1,128]{2,0,1:T(8,128)S(1)}, u32[]{:S(2)}, u32[]{:S(2)}) collective-permute-start(f32[128,1,128]{2,0,1:T(8,128)S(1)} %fusion.155), channel_id=1, source_target_pairs={{1020,0},{0,4},{4,8},{8,12},{12,16},{16,20},{20,24},{24,28},{28,32... | collective-permute-start | bytes 196616 | tf_op jit(solution)/shard_map/while/body/eval_jaxpr/ppermute | solution.py:26
  184.6 7.9 %collective-permute-start.3 = (f32[128,1,128]{2,0,1:T(8,128)S(1)}, f32[128,1,128]{2,0,1:T(8,128)S(1)}, u32[]{:S(2)}, u32[]{:S(2)}) collective-permute-start(f32[128,1,128]{2,0,1:T(8,128)S(1)} %fusion.154), channel_id=1, source_target_pairs={{1020,0},{0,4},{4,8},{8,12},{12,16},{16,20},{20,24},{24,28},{28,32... | collective-permute-start | bytes 196616 | tf_op jit(solution)/shard_map/while/body/eval_jaxpr/ppermute | solution.py:26
  186.7 6.3 %collective-permute-start.4 = (f32[128,1,128]{2,0,1:T(8,128)S(1)}, f32[128,1,128]{2,0,1:T(8,128)S(1)}, u32[]{:S(2)}, u32[]{:S(2)}) collective-permute-start(f32[128,1,128]{2,0,1:T(8,128)S(1)} %fusion.155), channel_id=1, source_target_pairs={{1020,0},{0,4},{4,8},{8,12},{12,16},{16,20},{20,24},{24,28},{28,32... | collective-permute-start | bytes 196616 | tf_op jit(solution)/shard_map/while/body/eval_jaxpr/ppermute | solution.py:26
  198.9 9.3 %collective-permute-start.3 = (f32[128,1,128]{2,0,1:T(8,128)S(1)}, f32[128,1,128]{2,0,1:T(8,128)S(1)}, u32[]{:S(2)}, u32[]{:S(2)}) collective-permute-start(f32[128,1,128]{2,0,1:T(8,128)S(1)} %fusion.154), channel_id=1, source_target_pairs={{1020,0},{0,4},{4,8},{8,12},{12,16},{16,20},{20,24},{24,28},{28,32... | collective-permute-start | bytes 196616 | tf_op jit(solution)/shard_map/while/body/eval_jaxpr/ppermute | solution.py:26
  201.5 7.3 %collective-permute-start.4 = (f32[128,1,128]{2,0,1:T(8,128)S(1)}, f32[128,1,128]{2,0,1:T(8,128)S(1)}, u32[]{:S(2)}, u32[]{:S(2)}) collective-permute-start(f32[128,1,128]{2,0,1:T(8,128)S(1)} %fusion.155), channel_id=1, source_target_pairs={{1020,0},{0,4},{4,8},{8,12},{12,16},{16,20},{20,24},{24,28},{28,32... | collective-permute-start | bytes 196616 | tf_op jit(solution)/shard_map/while/body/eval_jaxpr/ppermute | solution.py:26
  214.7 9.3 %collective-permute-start.3 = (f32[128,1,128]{2,0,1:T(8,128)S(1)}, f32[128,1,128]{2,0,1:T(8,128)S(1)}, u32[]{:S(2)}, u32[]{:S(2)}) collective-permute-start(f32[128,1,128]{2,0,1:T(8,128)S(1)} %fusion.154), channel_id=1, source_target_pairs={{1020,0},{0,4},{4,8},{8,12},{12,16},{16,20},{20,24},{24,28},{28,32... | collective-permute-start | bytes 196616 | tf_op jit(solution)/shard_map/while/body/eval_jaxpr/ppermute | solution.py:26
  217.3 7.3 %collective-permute-start.4 = (f32[128,1,128]{2,0,1:T(8,128)S(1)}, f32[128,1,128]{2,0,1:T(8,128)S(1)}, u32[]{:S(2)}, u32[]{:S(2)}) collective-permute-start(f32[128,1,128]{2,0,1:T(8,128)S(1)} %fusion.155), channel_id=1, source_target_pairs={{1020,0},{0,4},{4,8},{8,12},{12,16},{16,20},{20,24},{24,28},{28,32... | collective-permute-start | bytes 196616 | tf_op jit(solution)/shard_map/while/body/eval_jaxpr/ppermute | solution.py:26
  230.5 9.3 %collective-permute-start.3 = (f32[128,1,128]{2,0,1:T(8,128)S(1)}, f32[128,1,128]{2,0,1:T(8,128)S(1)}, u32[]{:S(2)}, u32[]{:S(2)}) collective-permute-start(f32[128,1,128]{2,0,1:T(8,128)S(1)} %fusion.154), channel_id=1, source_target_pairs={{1020,0},{0,4},{4,8},{8,12},{12,16},{16,20},{20,24},{24,28},{28,32... | collective-permute-start | bytes 196616 | tf_op jit(solution)/shard_map/while/body/eval_jaxpr/ppermute | solution.py:26
  233.1 7.3 %collective-permute-start.4 = (f32[128,1,128]{2,0,1:T(8,128)S(1)}, f32[128,1,128]{2,0,1:T(8,128)S(1)}, u32[]{:S(2)}, u32[]{:S(2)}) collective-permute-start(f32[128,1,128]{2,0,1:T(8,128)S(1)} %fusion.155), channel_id=1, source_target_pairs={{1020,0},{0,4},{4,8},{8,12},{12,16},{16,20},{20,24},{24,28},{28,32... | collective-permute-start | bytes 196616 | tf_op jit(solution)/shard_map/while/body/eval_jaxpr/ppermute | solution.py:26
  246.3 9.3 %collective-permute-start.3 = (f32[128,1,128]{2,0,1:T(8,128)S(1)}, f32[128,1,128]{2,0,1:T(8,128)S(1)}, u32[]{:S(2)}, u32[]{:S(2)}) collective-permute-start(f32[128,1,128]{2,0,1:T(8,128)S(1)} %fusion.154), channel_id=1, source_target_pairs={{1020,0},{0,4},{4,8},{8,12},{12,16},{16,20},{20,24},{24,28},{28,32... | collective-permute-start | bytes 196616 | tf_op jit(solution)/shard_map/while/body/eval_jaxpr/ppermute | solution.py:26
  248.9 7.3 %collective-permute-start.4 = (f32[128,1,128]{2,0,1:T(8,128)S(1)}, f32[128,1,128]{2,0,1:T(8,128)S(1)}, u32[]{:S(2)}, u32[]{:S(2)}) collective-permute-start(f32[128,1,128]{2,0,1:T(8,128)S(1)} %fusion.155), channel_id=1, source_target_pairs={{1020,0},{0,4},{4,8},{8,12},{12,16},{16,20},{20,24},{24,28},{28,32... | collective-permute-start | bytes 196616 | tf_op jit(solution)/shard_map/while/body/eval_jaxpr/ppermute | solution.py:26
  262.0 9.3 %collective-permute-start.3 = (f32[128,1,128]{2,0,1:T(8,128)S(1)}, f32[128,1,128]{2,0,1:T(8,128)S(1)}, u32[]{:S(2)}, u32[]{:S(2)}) collective-permute-start(f32[128,1,128]{2,0,1:T(8,128)S(1)} %fusion.154), channel_id=1, source_target_pairs={{1020,0},{0,4},{4,8},{8,12},{12,16},{16,20},{20,24},{24,28},{28,32... | collective-permute-start | bytes 196616 | tf_op jit(solution)/shard_map/while/body/eval_jaxpr/ppermute | solution.py:26
  264.6 7.3 %collective-permute-start.4 = (f32[128,1,128]{2,0,1:T(8,128)S(1)}, f32[128,1,128]{2,0,1:T(8,128)S(1)}, u32[]{:S(2)}, u32[]{:S(2)}) collective-permute-start(f32[128,1,128]{2,0,1:T(8,128)S(1)} %fusion.155), channel_id=1, source_target_pairs={{1020,0},{0,4},{4,8},{8,12},{12,16},{16,20},{20,24},{24,28},{28,32... | collective-permute-start | bytes 196616 | tf_op jit(solution)/shard_map/while/body/eval_jaxpr/ppermute | solution.py:26
  277.8 9.3 %collective-permute-start.3 = (f32[128,1,128]{2,0,1:T(8,128)S(1)}, f32[128,1,128]{2,0,1:T(8,128)S(1)}, u32[]{:S(2)}, u32[]{:S(2)}) collective-permute-start(f32[128,1,128]{2,0,1:T(8,128)S(1)} %fusion.154), channel_id=1, source_target_pairs={{1020,0},{0,4},{4,8},{8,12},{12,16},{16,20},{20,24},{24,28},{28,32... | collective-permute-start | bytes 196616 | tf_op jit(solution)/shard_map/while/body/eval_jaxpr/ppermute | solution.py:26
  280.4 7.3 %collective-permute-start.4 = (f32[128,1,128]{2,0,1:T(8,128)S(1)}, f32[128,1,128]{2,0,1:T(8,128)S(1)}, u32[]{:S(2)}, u32[]{:S(2)}) collective-permute-start(f32[128,1,128]{2,0,1:T(8,128)S(1)} %fusion.155), channel_id=1, source_target_pairs={{1020,0},{0,4},{4,8},{8,12},{12,16},{16,20},{20,24},{24,28},{28,32... | collective-permute-start | bytes 196616 | tf_op jit(solution)/shard_map/while/body/eval_jaxpr/ppermute | solution.py:26
  293.6 9.3 %collective-permute-start.3 = (f32[128,1,128]{2,0,1:T(8,128)S(1)}, f32[128,1,128]{2,0,1:T(8,128)S(1)}, u32[]{:S(2)}, u32[]{:S(2)}) collective-permute-start(f32[128,1,128]{2,0,1:T(8,128)S(1)} %fusion.154), channel_id=1, source_target_pairs={{1020,0},{0,4},{4,8},{8,12},{12,16},{16,20},{20,24},{24,28},{28,32... | collective-permute-start | bytes 196616 | tf_op jit(solution)/shard_map/while/body/eval_jaxpr/ppermute | solution.py:26
  296.2 7.3 %collective-permute-start.4 = (f32[128,1,128]{2,0,1:T(8,128)S(1)}, f32[128,1,128]{2,0,1:T(8,128)S(1)}, u32[]{:S(2)}, u32[]{:S(2)}) collective-permute-start(f32[128,1,128]{2,0,1:T(8,128)S(1)} %fusion.155), channel_id=1, source_target_pairs={{1020,0},{0,4},{4,8},{8,12},{12,16},{16,20},{20,24},{24,28},{28,32... | collective-permute-start | bytes 196616 | tf_op jit(solution)/shard_map/while/body/eval_jaxpr/ppermute | solution.py:26
  309.3 9.3 %collective-permute-start.3 = (f32[128,1,128]{2,0,1:T(8,128)S(1)}, f32[128,1,128]{2,0,1:T(8,128)S(1)}, u32[]{:S(2)}, u32[]{:S(2)}) collective-permute-start(f32[128,1,128]{2,0,1:T(8,128)S(1)} %fusion.154), channel_id=1, source_target_pairs={{1020,0},{0,4},{4,8},{8,12},{12,16},{16,20},{20,24},{24,28},{28,32... | collective-permute-start | bytes 196616 | tf_op jit(solution)/shard_map/while/body/eval_jaxpr/ppermute | solution.py:26
  311.9 7.3 %collective-permute-start.4 = (f32[128,1,128]{2,0,1:T(8,128)S(1)}, f32[128,1,128]{2,0,1:T(8,128)S(1)}, u32[]{:S(2)}, u32[]{:S(2)}) collective-permute-start(f32[128,1,128]{2,0,1:T(8,128)S(1)} %fusion.155), channel_id=1, source_target_pairs={{1020,0},{0,4},{4,8},{8,12},{12,16},{16,20},{20,24},{24,28},{28,32... | collective-permute-start | bytes 196616 | tf_op jit(solution)/shard_map/while/body/eval_jaxpr/ppermute | solution.py:26
  319.2 16.5 %copy-start.4 = (f32[1,8,128,128]{2,3,1,0:T(8,128)S(1)}, f32[1,8,128,128]{2,3,1,0:T(8,128)}, u32[]{:S(2)}) copy-start(f32[1,8,128,128]{2,3,1,0:T(8,128)} %copy-done.3) | copy-start | bytes 1572868
  319.2 16.5 %copy-start.5 = (bf16[128,1024]{1,0:T(8,128)(2,1)S(1)}, bf16[128,1024]{1,0:T(8,128)(2,1)}, u32[]{:S(2)}) copy-start(bf16[128,1024]{1,0:T(8,128)(2,1)} %param.17) | copy-start | bytes 786436
  319.2 18.9 %copy-start.2 = (bf16[128,128]{0,1:T(8,128)(2,1)S(1)}, bf16[128,128]{0,1:T(8,128)(2,1)}, u32[]{:S(2)}) copy-start(bf16[128,128]{0,1:T(8,128)(2,1)} %copy-done.1) | copy-start | bytes 98308
  319.2 18.9 %copy-start.7 = (f32[128]{0:T(128)S(1)}, f32[128]{0:T(128)}, u32[]{:S(2)}) copy-start(f32[128]{0:T(128)} %param.19) | copy-start | bytes 1540
  319.2 19.0 %copy-start.11 = (f32[128]{0:T(128)S(1)}, f32[128]{0:T(128)}, u32[]{:S(2)}) copy-start(f32[128]{0:T(128)} %copy-done.10) | copy-start | bytes 1540
  319.2 19.0 %copy-start.9 = (f32[128]{0:T(128)S(1)}, f32[128]{0:T(128)}, u32[]{:S(2)}) copy-start(f32[128]{0:T(128)} %copy-done.8) | copy-start | bytes 1540
  327.3 10.8 %collective-permute-start.5 = (bf16[128,1,128]{0,2,1:T(8,128)(2,1)S(1)}, bf16[128,1,128]{0,2,1:T(8,128)(2,1)S(1)}, u32[]{:S(2)}, u32[]{:S(2)}) collective-permute-start(bf16[128,1,128]{0,2,1:T(8,128)(2,1)S(1)} %fusion.73), channel_id=1, source_target_pairs={{40,0},{44,4},{48,8},{52,12},{56,16},{60,20},{64,24},{68,28},{72,3... | collective-permute-start | bytes 98312 | tf_op jit(solution)/shard_map/ppermute | solution.py:26
  336.0 8.8 %collective-permute-start.6 = (bf16[128,1,128]{2,0,1:T(8,128)(2,1)S(1)}, bf16[128,1,128]{2,0,1:T(8,128)(2,1)S(1)}, u32[]{:S(2)}, u32[]{:S(2)}) collective-permute-start(bf16[128,1,128]{2,0,1:T(8,128)(2,1)S(1)} %fusion.74), channel_id=1, source_target_pairs={{40,0},{44,4},{48,8},{52,12},{56,16},{60,20},{64,24},{68,28},{72,3... | collective-permute-start | bytes 98312 | tf_op jit(solution)/shard_map/ppermute | solution.py:26
  (3 other events, 8.4 us)
Sparse Core Ops, SparseCore 0:
  327.1 57.6 reduce-scatter.1
where the time goes:
time: 395 us; the launch traced here: 392 us
  starting transfers between devices  183 us (46%)
  loops' own time  60.7 us (15%)
  waiting for transfers between devices  52.8 us (13%)
  local copies, waits for them, and re-layouts  45.1 us (11%)
  matrix products  29.5 us (7%)
  between operations  15.1 us (4%)
  other arithmetic  5.87 us (1%)
    ppermute x22, starting transfers between devices, from_behind(): return lax.ppermute(block, axis, route)  92.6 us
    ppermute x30, starting transfers between devices, passed_along(): return lax.ppermute(array, axis, pairs)  90.5 us
    reduce_scatter x1, waiting for transfers between devices, local(): lax.psum_scatter(term.astype(jnp.bfloat16), 'head', scatter_dimension=1,...  40 us
    another operation x1, loops' own time, local(): lax.scan(relay_step, ((zero_kv, zero_kv), zero_weighted), jnp.arange(HOPS...  39.8 us
    another operation x1, loops' own time, local(): lax.scan(forward_step, (start_block, zero_total, zero_weighted), jnp.aran...  20.9 us
    dynamic_update_slice x20, local copies, waits for them, and re-layouts, local(): lax.scan(forward_step, (start_block, zero_total, zero_weighted), jnp.aran...  19.8 us
    ppermute x22, waiting for transfers between devices, from_behind(): return lax.ppermute(block, axis, route)  12.7 us
    dynamic_slice x20, local copies, waits for them, and re-layouts, local(): lax.scan(forward_step, (start_block, zero_total, zero_weighted), jnp.aran...  11.6 us
  transfers between devices with their start and end apart: 53, of which 13 were waited for; matrix products, arithmetic and copies ran while one was open for 10% of the time, Pallas kernels for 0%

commit v1 on v0

v1 whole, which is shorter than its diff:
```python
import functools

import jax
import jax.numpy as jnp
from jax import lax
from jax.experimental import pallas as pl
from jax.experimental.pallas import tpu as pltpu
from jax.sharding import PartitionSpec as P

HD = 128
BLOCK = 128
HOPS = 10
NBUCKET = 16
PAIR = 2
BACK = HOPS // PAIR
NCH = BACK + 1
KEYS = PAIR * BLOCK
KVROWS = 2 * BLOCK + 16
EPS = 1e-06
MESH = pl.DeviceIdType.MESH
F32 = jnp.float32
BF16 = jnp.bfloat16
EXP2_SCALE = (HD**-0.5) * 1.4426950408889634


def dot(a, b):
    return jnp.dot(a, b, preferred_element_type=F32)


def dot_t(a, b):
    return lax.dot_general(a, b, (((0,), (0,)), ((), ())), preferred_element_type=F32)


def kernel(
    n_ctx,
    n_head,
    heads,
    bucket_ref,
    table_ref,
    doc_ref,
    qgain_ref,
    kgain_ref,
    q_hbm,
    k_hbm,
    v_hbm,
    g_hbm,
    w_hbm,
    gi_ref,
    gk_ref,
    gv_ref,
    q_ref,
    k_ref,
    v_ref,
    g_ref,
    w_ref,
    kvb,
    mask,
    qt,
    rq,
    qhat,
    qhat_t,
    g_t,
    gs,
    gs_t,
    delta,
    total,
    out_t,
    expo,
    ds,
    dq_t,
    dqr_t,
    part_tmp,
    part_own,
    part_out,
    part_in,
    comb,
    arrived,
    term_out,
    relay_in,
    term_in,
    in_sem,
    kv_send,
    kv_recv,
    fw_send,
    fw_recv,
    pt_send,
    pt_recv,
    cb_send,
    cb_recv,
    rs_send,
    rs_recv,
):
    me = lax.axis_index("ctx")
    hx = lax.axis_index("head")
    core = lax.rem(me, PAIR)
    sib = me + 1 - 2 * core
    other = 1 - core
    width = gi_ref.shape[1]
    half = width // 2
    pairs = heads // 2

    def ctx_at(step):
        return lax.rem(me + step * PAIR + n_ctx, n_ctx)

    def head_at(step):
        return lax.rem(hx + step + n_head, n_head)

    loads = [
        pltpu.make_async_copy(k_hbm, k_ref, in_sem.at[0]),
        pltpu.make_async_copy(v_hbm, v_ref, in_sem.at[1]),
        pltpu.make_async_copy(q_hbm, q_ref, in_sem.at[2]),
        pltpu.make_async_copy(g_hbm, g_ref, in_sem.at[3]),
        pltpu.make_async_copy(w_hbm, w_ref, in_sem.at[4]),
    ]
    for copy in loads:
        copy.start()

    barrier = pltpu.get_barrier_semaphore()
    peers = [(sib, hx), (me, head_at(1)), (me, head_at(-1))]
    for step in range(1, BACK + 1):
        peers += [(ctx_at(step), hx), (ctx_at(-step), hx)]
    for peer in peers:
        pl.semaphore_signal(barrier, inc=1, device_id=peer, device_id_type=MESH)

    own_doc = doc_ref[0].astype(F32)
    loads[0].wait()
    loads[1].wait()
    k_f = k_ref[...].astype(F32)
    k_r = lax.rsqrt(jnp.mean(k_f * k_f, axis=-1, keepdims=True) + EPS)
    kvb[0, core, 0:BLOCK, :] = (k_f * k_r * kgain_ref[...]).astype(BF16)
    kvb[0, core, BLOCK : 2 * BLOCK, :] = v_ref[...]
    kvb[0, core, 2 * BLOCK : KVROWS, :] = jnp.full((16, HD), own_doc, F32).astype(BF16)
    pl.semaphore_wait(barrier, len(peers))

    sends = []

    def send(src, dst, send_sem, recv_sem, target):
        copy = pltpu.make_async_remote_copy(
            src_ref=src,
            dst_ref=dst,
            send_sem=send_sem,
            recv_sem=recv_sem,
            device_id=target,
            device_id_type=MESH,
        )
        copy.start()
        sends.append(copy)
        return copy

    own_kv = kvb.at[0, core]
    fw = [send(own_kv, own_kv, fw_send.at[0], fw_recv.at[0], (sib, hx))]
    kv = [None]
    for j in range(1, NCH):
        kv.append(
            send(own_kv, kvb.at[j, core], kv_send.at[j], kv_recv.at[j], (ctx_at(j), hx))
        )

    weight = jnp.zeros((1, BLOCK), F32)
    for b in range(NBUCKET):
        weight = jnp.where(bucket_ref[...] == b, table_ref[b], weight)
    gain_t = jnp.broadcast_to(qgain_ref[...], (HD, HD)).T
    loads[2].wait()
    for h in range(heads):
        cols = pl.ds(h * HD, HD)
        x_t = q_ref[:, cols].T
        qt[cols, :] = x_t
        x = x_t.astype(F32)
        r = lax.rsqrt(jnp.mean(x * x, axis=0, keepdims=True) + EPS)
        rq[h : h + 1, :] = r
        hat = (x * r * gain_t).astype(BF16)
        qhat_t[:, cols] = hat
        qhat[cols, :] = hat.T
    loads[3].wait()
    for h in range(heads):
        cols = pl.ds(h * HD, HD)
        g_t[:, cols] = g_ref[:, cols].T

    key_pos = lax.broadcasted_iota(jnp.int32, (KEYS, BLOCK), 0)
    row_pos = lax.broadcasted_iota(jnp.int32, (KEYS, BLOCK), 1) + core * BLOCK
    causal = jnp.where(key_pos <= row_pos, 1.0, 0.0)

    for j in range(NCH):
        if j > 0:
            kv[j].wait_recv()
            slot = kvb.at[j, core]
            fw.append(send(slot, slot, fw_send.at[j], fw_recv.at[j], (sib, hx)))
        fw[j].wait_recv()
        for b in range(PAIR):
            docs = kvb[j, b, 2 * BLOCK : KVROWS, :].astype(F32)[0:1]
            same = jnp.where(docs == own_doc, 1.0, 0.0)
            rows = slice(b * BLOCK, (b + 1) * BLOCK)
            if j == 0:
                mask[rows, :] = causal[rows] * same
            else:
                mask[rows, :] = jnp.broadcast_to(same, (BLOCK, BLOCK))
        keys = jnp.concatenate([kvb[j, b, 0:BLOCK, :] for b in range(PAIR)], axis=0)
        vals = jnp.concatenate([kvb[j, b, BLOCK : 2 * BLOCK, :] for b in range(PAIR)], axis=0)
        for p in range(pairs):
            cols = pl.ds(p * KEYS, KEYS)
            s = dot(keys, qhat_t[:, cols])
            m = mask[...]
            e = jnp.exp2(s * EXP2_SCALE) * jnp.concatenate([m, m], axis=1)
            part = jnp.sum(e.reshape(KEYS // 8, 8, KEYS), axis=0)
            e_half = e.astype(BF16)
            expo[j, :, cols] = e_half
            weighted = dot_t(vals, e_half)
            if j == 0:
                total[:, cols] = part
                out_t[:, cols] = weighted
            else:
                total[:, cols] += part
                out_t[:, cols] += weighted

    for p in range(pairs):
        cols = pl.ds(p * KEYS, KEYS)
        inv = 1.0 / jnp.sum(total[:, cols], axis=0, keepdims=True)
        scaled = (g_t[:, cols].astype(F32) * (jnp.concatenate([weight, weight], axis=1) * inv)).astype(BF16)
        gs_t[:, cols] = scaled
        gs[cols, :] = scaled.T
        delta[:, cols] = jnp.broadcast_to(
            jnp.sum(scaled.astype(F32) * out_t[:, cols], axis=0, keepdims=True) * inv, (8, KEYS)
        )

    mine = pl.ds(pl.multiple_of(core * BLOCK, BLOCK), BLOCK)
    theirs = pl.ds(pl.multiple_of(other * BLOCK, BLOCK), BLOCK)
    pt = [None] * NCH
    cb = [None] * NCH

    def pass_on(j):
        pt[j].wait_recv()
        both = part_own[j] + part_in[j].astype(F32)
        if j > 0:
            comb[j] = both.astype(BF16)
            cb[j] = send(comb.at[j], arrived.at[j], cb_send.at[j], cb_recv.at[j], (ctx_at(-j), hx))
        else:
            part_own[0] = both

    order = list(range(NCH - 1, -1, -1))
    for n, j in enumerate(order):
        keys = jnp.concatenate([kvb[j, b, 0:BLOCK, :] for b in range(PAIR)], axis=0)
        vals = jnp.concatenate([kvb[j, b, BLOCK : 2 * BLOCK, :] for b in range(PAIR)], axis=0)
        for p in range(pairs):
            cols = pl.ds(p * KEYS, KEYS)
            gv = dot(vals, gs_t[:, cols])
            e = expo[j, :, cols].astype(F32)
            d = (e * (gv - delta[0:1, cols])).astype(BF16)
            ds[:, cols] = d
            dq = dot_t(keys, d)
            if n == 0:
                dq_t[:, cols] = dq
            else:
                dq_t[:, cols] += dq
        part_tmp[0] = dot(ds[...], qhat[...])
        part_tmp[1] = dot(expo[j], gs[...])
        for i in range(2):
            rows = slice(i * BLOCK, (i + 1) * BLOCK)
            part_own[j, rows, :] = part_tmp[i, mine, :]
            part_out[j, rows, :] = part_tmp[i, theirs, :].astype(BF16)
        pt[j] = send(part_out.at[j], part_in.at[j], pt_send.at[j], pt_recv.at[j], (sib, hx))
        if n > 0:
            pass_on(order[n - 1])

    for h in range(heads):
        cols = pl.ds(h * HD, HD)
        r = rq[h : h + 1, :]
        xn = qt[cols, :].astype(F32) * r
        gc = gain_t * (dq_t[:, cols] * (HD**-0.5))
        back = r * (gc - xn * jnp.mean(xn * gc, axis=0, keepdims=True))
        dqr_t[cols, :] = back.astype(BF16)

    loads[4].wait()

    def term(step, part):
        first = pl.multiple_of(head_at(step) * width + part * half, half)
        return dot(w_ref[pl.ds(first, half), :], dqr_t[...])

    def hand(slot, value, dst, recv, step):
        term_out[slot] = value.astype(BF16)
        return send(term_out.at[slot], dst, rs_send.at[slot], rs_recv.at[recv], (me, head_at(step)))

    up_relay = hand(0, term(2, 0), relay_in.at[0], 0, 1)
    down_relay = hand(1, term(2, 1), relay_in.at[1], 1, -1)
    direct_up = hand(2, term(1, 1), term_in.at[0, 1], 2, 1)
    direct_down = hand(3, term(-1, 0), term_in.at[1, 0], 3, -1)
    part = term(1, 0)
    up_relay.wait_recv()
    summed_up = hand(4, part + relay_in[0].astype(F32), term_in.at[0, 0], 4, 1)
    part = term(-1, 1)
    down_relay.wait_recv()
    summed_down = hand(5, part + relay_in[1].astype(F32), term_in.at[1, 1], 5, -1)
    own = [term(0, 0), term(0, 1)]

    pass_on(0)
    dkv = part_own[0]
    for j in range(NCH - 1, 0, -1):
        cb[j].wait_recv()
        dkv = dkv + arrived[j].astype(F32)
    gv_ref[...] = dkv[BLOCK:].astype(BF16)
    k_f = k_ref[...].astype(F32)
    k_r = lax.rsqrt(jnp.mean(k_f * k_f, axis=-1, keepdims=True) + EPS)
    xn = k_f * k_r
    gc = kgain_ref[...] * (dkv[:BLOCK] * (HD**-0.5))
    gk_ref[...] = (k_r * (gc - xn * jnp.mean(xn * gc, axis=-1, keepdims=True))).astype(BF16)

    for i, arrivals in enumerate(((summed_up, direct_down), (direct_up, summed_down))):
        for copy in arrivals:
            copy.wait_recv()
        sum_t = own[i] + term_in[0, i].astype(F32) + term_in[1, i].astype(F32)
        for b in range(half // BLOCK):
            first = i * half + b * BLOCK
            gi_ref[:, first : first + BLOCK] = sum_t[b * BLOCK : (b + 1) * BLOCK].T.astype(BF16)

    for copy in sends:
        copy.wait_send()


def local(mesh, *args):
    q, k, v, g, q_gain, k_gain, table, bucket, docs, w = args
    n_ctx, n_head = mesh.shape["ctx"], mesh.shape["head"]
    tokens, features = q.shape
    heads = features // HD
    cols = heads * BLOCK
    width = w.shape[0] // n_head
    half = width // 2
    vmem = pl.BlockSpec(memory_space=pltpu.VMEM)
    smem = pl.BlockSpec(memory_space=pltpu.SMEM)
    hbm = pl.BlockSpec(memory_space=pl.ANY)
    dma = pltpu.SemaphoreType.DMA
    return pl.pallas_call(
        functools.partial(kernel, n_ctx, n_head, heads),
        out_shape=(
            jax.ShapeDtypeStruct((tokens, width), BF16),
            jax.ShapeDtypeStruct(k.shape, BF16),
            jax.ShapeDtypeStruct(v.shape, BF16),
        ),
        in_specs=[vmem, smem, smem, vmem, vmem, hbm, hbm, hbm, hbm, hbm],
        out_specs=(vmem, vmem, vmem),
        scratch_shapes=[
            pltpu.VMEM(q.shape, BF16),
            pltpu.VMEM(k.shape, BF16),
            pltpu.VMEM(v.shape, BF16),
            pltpu.VMEM(g.shape, BF16),
            pltpu.VMEM(w.shape, BF16),
            pltpu.VMEM((NCH, PAIR, KVROWS, HD), BF16),
            pltpu.VMEM((KEYS, BLOCK), F32),
            pltpu.VMEM((cols, BLOCK), BF16),
            pltpu.VMEM((heads, BLOCK), F32),
            pltpu.VMEM((cols, HD), BF16),
            pltpu.VMEM((HD, cols), BF16),
            pltpu.VMEM((HD, cols), BF16),
            pltpu.VMEM((cols, HD), BF16),
            pltpu.VMEM((HD, cols), BF16),
            pltpu.VMEM((8, cols), F32),
            pltpu.VMEM((8, cols), F32),
            pltpu.VMEM((HD, cols), F32),
            pltpu.VMEM((NCH, KEYS, cols), BF16),
            pltpu.VMEM((KEYS, cols), BF16),
            pltpu.VMEM((HD, cols), F32),
            pltpu.VMEM((cols, BLOCK), BF16),
            pltpu.VMEM((2, KEYS, HD), F32),
            pltpu.VMEM((NCH, 2 * BLOCK, HD), F32),
            pltpu.VMEM((NCH, 2 * BLOCK, HD), BF16),
            pltpu.VMEM((NCH, 2 * BLOCK, HD), BF16),
            pltpu.VMEM((NCH, 2 * BLOCK, HD), BF16),
            pltpu.VMEM((NCH, 2 * BLOCK, HD), BF16),
            pltpu.VMEM((6, half, BLOCK), BF16),
            pltpu.VMEM((2, half, BLOCK), BF16),
            pltpu.VMEM((2, 2, half, BLOCK), BF16),
            dma((5,)),
            dma((NCH,)),
            dma((NCH,)),
            dma((NCH,)),
            dma((NCH,)),
            dma((NCH,)),
            dma((NCH,)),
            dma((NCH,)),
            dma((NCH,)),
            dma((6,)),
            dma((6,)),
        ],
        compiler_params=pltpu.CompilerParams(
            collective_id=0, has_side_effects=True, vmem_limit_bytes=56 * 1024 * 1024
        ),
    )(bucket.reshape(1, tokens), table, docs, q_gain.reshape(1, HD), k_gain.reshape(1, HD), q, k, v, g, w)


def solution(mesh):
    placed = (
        P("ctx", "head"),
        P("ctx", "head"),
        P("ctx", "head"),
        P("ctx", "head"),
        P(),
        P(),
        P(),
        P("ctx"),
        P("ctx"),
        P(None, "head"),
    )
    return jax.shard_map(
        functools.partial(local, mesh),
        mesh=mesh,
        in_specs=placed,
        out_specs=(P("ctx", "head"), P("ctx", "head"), P("ctx", "head")),
        check_vma=False,
    )
```

time: 395 us -> 65.1 us (0.16)
  the two profiles are of different devices: /device:TPU:24 before, /device:TPU:8 now
where the time goes in v1:
time: 65.1 us; the launch traced here: 64.7 us
  Pallas kernels  59 us (91%)
  local copies, waits for them, and re-layouts  4.42 us (7%)
  between operations  1.29 us (2%)
    pallas_call x1, Pallas kernels, local(): pl.pallas_call(functools.partial(kernel, n_ctx, n_head, heads), out_shape...  59 us
    unnamed x3, local copies, waits for them, and re-layouts  4.42 us

profile of v1, /device:TPU:8, one launch (start us, length us, event | category | flops | bytes accessed | tf_op | source)
XLA Modules:
  0.0 64.7 jit_solution(12603039627197371115)
XLA Ops:
  1.3 59.0 %shard_map.121 = (bf16[128,1024]{1,0:T(8,128)(2,1)}, bf16[128,128]{1,0:T(8,128)(2,1)}, bf16[128,128]{1,0:T(8,128)(2,1)}) custom-call(s32[1,128]{1,0:T(1,128)} %bitcast.3, f32[16]{0:T(128)} %table_ref.1, s32[1]{0:T(128)S(6)} %copy.16.doc_ref, f32[1,128]{1,0:T(1,128)} %bitcast.4, f32[1,128]{1,0:T(1,128)} %bitcast.5, bf16[128,1024]{1,0:T(8,128)(2,1)} %q_hbm.1, ...), custom_call_target="tpu_custom_call" | custom-call | tf_op jit(solution)/shard_map/pallas_call | solution.py:329
  60.3 1.7 %copy.17 = bf16[128,1024]{1,0:T(8,128)(2,1)} copy(bf16[128,1024]{1,0:T(8,128)(2,1)} %get-tuple-element.6) | data formatting | bytes 524288
  62.0 1.4 %copy.18 = bf16[128,128]{1,0:T(8,128)(2,1)} copy(bf16[128,128]{1,0:T(8,128)(2,1)} %get-tuple-element.7) | data formatting | bytes 65536
  63.4 1.4 %copy.19 = bf16[128,128]{1,0:T(8,128)(2,1)} copy(bf16[128,128]{1,0:T(8,128)(2,1)} %get-tuple-element.8) | data formatting | bytes 65536

commit v2 on v1

v2 whole, which is shorter than its diff:
```python
import functools

import jax
import jax.numpy as jnp
from jax import lax
from jax.experimental import pallas as pl
from jax.experimental.pallas import tpu as pltpu
from jax.sharding import PartitionSpec as P

HD = 128
BLOCK = 128
HOPS = 10
NBUCKET = 16
PAIR = 2
BACK = HOPS // PAIR
NCH = BACK + 1
KEYS = PAIR * BLOCK
KVROWS = 2 * BLOCK + 16
EPS = 1e-06
MESH = pl.DeviceIdType.MESH
F32 = jnp.float32
BF16 = jnp.bfloat16
EXP2_SCALE = (HD**-0.5) * 1.4426950408889634


def dot(a, b):
    return jnp.dot(a, b, preferred_element_type=F32)


def dot_nt(a, b):
    return lax.dot_general(a, b, (((1,), (1,)), ((), ())), preferred_element_type=F32)


def dot_t(a, b):
    return lax.dot_general(a, b, (((0,), (0,)), ((), ())), preferred_element_type=F32)


def kernel(
    n_ctx,
    n_head,
    heads,
    bucket_ref,
    table_ref,
    doc_ref,
    qgain_ref,
    kgain_ref,
    q_hbm,
    k_hbm,
    v_hbm,
    g_hbm,
    w_hbm,
    gi_ref,
    gk_ref,
    gv_ref,
    doc_s,
    q_ref,
    k_ref,
    v_ref,
    g_ref,
    w_ref,
    kvb,
    mask,
    qt,
    rq,
    qhat_t,
    g_t,
    gs_t,
    rows_of,
    total,
    out_t,
    expo,
    prods,
    ds,
    dq_t,
    dqr_t,
    part_tmp,
    part_own,
    part_out,
    part_in,
    comb,
    arrived,
    term_out,
    relay_in,
    term_in,
    in_sem,
    kv_send,
    kv_recv,
    fw_send,
    fw_recv,
    pt_send,
    pt_recv,
    cb_send,
    cb_recv,
    rs_send,
    rs_recv,
):
    me = lax.axis_index("ctx")
    hx = lax.axis_index("head")
    core = lax.rem(me, PAIR)
    sib = me + 1 - 2 * core
    other = 1 - core
    width = gi_ref.shape[1]
    half = width // 2
    pairs = heads // 2

    chip = lax.div(me, PAIR)
    chips = n_ctx // PAIR

    def has_back(step):
        return chip >= step

    def has_next(step):
        return chip + step < chips

    def ctx_at(step):
        return me + step * PAIR

    def head_at(step):
        return lax.rem(hx + step + n_head, n_head)

    loads = [
        pltpu.make_async_copy(k_hbm, k_ref, in_sem.at[0]),
        pltpu.make_async_copy(v_hbm, v_ref, in_sem.at[1]),
        pltpu.make_async_copy(q_hbm, q_ref, in_sem.at[2]),
        pltpu.make_async_copy(g_hbm, g_ref, in_sem.at[3]),
        pltpu.make_async_copy(w_hbm, w_ref, in_sem.at[4]),
        pltpu.make_async_copy(doc_ref, doc_s, in_sem.at[5]),
    ]
    for i in (0, 1, 5, 2, 3, 4):
        loads[i].start()

    barrier = pltpu.get_barrier_semaphore()

    def greet(target):
        pl.semaphore_signal(barrier, inc=1, device_id=target, device_id_type=MESH)

    for peer in [(sib, hx), (me, head_at(1)), (me, head_at(-1))]:
        greet(peer)
    for step in range(1, BACK + 1):

        @pl.when(has_next(step))
        def _():
            greet((ctx_at(step), hx))

        @pl.when(has_back(step))
        def _():
            greet((ctx_at(-step), hx))

    loads[5].wait()
    own_doc = jnp.full((1, HD), doc_s[0], jnp.int32).astype(F32)
    loads[0].wait()
    loads[1].wait()
    k_f = k_ref[...].astype(F32)
    k_r = lax.rsqrt(jnp.mean(k_f * k_f, axis=-1, keepdims=True) + EPS)
    kvb[0, core, 0:BLOCK, :] = (k_f * k_r * kgain_ref[...]).astype(BF16)
    kvb[0, core, BLOCK : 2 * BLOCK, :] = v_ref[...]
    kvb[0, core, 2 * BLOCK : KVROWS, :] = jnp.broadcast_to(own_doc, (16, HD)).astype(BF16)
    pl.semaphore_wait(barrier, 3 + jnp.minimum(chip, BACK) + jnp.minimum(chips - 1 - chip, BACK))

    sends = []

    def remote(src, dst, send_sem, recv_sem, target):
        return pltpu.make_async_remote_copy(
            src_ref=src,
            dst_ref=dst,
            send_sem=send_sem,
            recv_sem=recv_sem,
            device_id=target,
            device_id_type=MESH,
        )

    def send(src, dst, send_sem, recv_sem, target):
        copy = remote(src, dst, send_sem, recv_sem, target)
        copy.start()
        sends.append((copy, None))
        return copy

    def send_if(cond, src, dst, send_sem, recv_sem, target):
        copy = remote(src, dst, send_sem, recv_sem, target)
        pl.when(cond)(copy.start)
        sends.append((copy, cond))
        return copy

    own_kv = kvb.at[0, core]
    fw = [send(own_kv, own_kv, fw_send.at[0], fw_recv.at[0], (sib, hx))]
    for j in range(1, NCH):
        slot = kvb.at[j, core]
        fw.append(remote(slot, slot, fw_send.at[j], fw_recv.at[j], (sib, hx)))
        sends.append((fw[j], has_back(j)))
    kv = [None]
    for j in range(1, NCH):
        kv.append(
            send_if(has_next(j), own_kv, kvb.at[j, core], kv_send.at[j], kv_recv.at[j], (ctx_at(j), hx))
        )

    weight = jnp.zeros((1, BLOCK), F32)
    for b in range(NBUCKET):
        weight = jnp.where(bucket_ref[...] == b, table_ref[b], weight)
    gain_t = jnp.broadcast_to(qgain_ref[...], (HD, HD)).T
    loads[2].wait()
    for h in range(heads):
        cols = pl.ds(h * HD, HD)
        x_t = q_ref[:, cols].T
        qt[cols, :] = x_t
        x = x_t.astype(F32)
        r = lax.rsqrt(jnp.mean(x * x, axis=0, keepdims=True) + EPS)
        rq[h : h + 1, :] = r
        qhat_t[:, cols] = (x * r * gain_t).astype(BF16)
    loads[3].wait()
    for h in range(heads):
        cols = pl.ds(h * HD, HD)
        g_t[:, cols] = g_ref[:, cols].T

    key_pos = lax.broadcasted_iota(jnp.int32, (KEYS, BLOCK), 0)
    row_pos = lax.broadcasted_iota(jnp.int32, (KEYS, BLOCK), 1) + core * BLOCK
    causal = jnp.where(key_pos <= row_pos, 1.0, 0.0)

    def both(j, first):
        return jnp.concatenate([kvb[j, b, first : first + BLOCK, :] for b in range(PAIR)], axis=0)

    def first_pass(j):
        if j > 0:
            kv[j].wait_recv()
            fw[j].start()
        fw[j].wait_recv()
        for b in range(PAIR):
            docs = kvb[j, b, 2 * BLOCK : KVROWS, :].astype(F32)[0:1]
            same = jnp.where(docs == own_doc, 1.0, 0.0)
            rows = slice(b * BLOCK, (b + 1) * BLOCK)
            if j == 0:
                mask[rows, :] = causal[rows] * same
            else:
                mask[rows, :] = jnp.broadcast_to(same, (BLOCK, BLOCK))
        keys, vals = both(j, 0), both(j, BLOCK)
        for p in range(pairs):
            cols = pl.ds(p * KEYS, KEYS)
            s = dot(keys, qhat_t[:, cols])
            m = mask[...]
            e = jnp.exp2(s * EXP2_SCALE) * jnp.concatenate([m, m], axis=1)
            part = jnp.sum(e.reshape(KEYS // 8, 8, KEYS), axis=0)
            e_half = e.astype(BF16)
            expo[j, :, cols] = e_half
            prods[j, :, cols] = dot(vals, g_t[:, cols])
            weighted = dot_t(vals, e_half)
            if j == 0:
                total[:, cols] = part
                out_t[:, cols] = weighted
            else:
                total[:, cols] += part
                out_t[:, cols] += weighted

    for j in range(NCH):
        if j == 0:
            first_pass(0)
        else:
            pl.when(has_back(j))(functools.partial(first_pass, j))

    for p in range(pairs):
        cols = pl.ds(p * KEYS, KEYS)
        inv = 1.0 / jnp.sum(total[:, cols], axis=0, keepdims=True)
        ratio = jnp.concatenate([weight, weight], axis=1) * inv
        g = g_t[:, cols].astype(F32)
        gs_t[:, cols] = (g * ratio).astype(BF16)
        rows_of[0:1, cols] = ratio
        rows_of[1:2, cols] = jnp.sum(g * out_t[:, cols], axis=0, keepdims=True) * (inv * ratio)

    def second_pass(j):
        keys = both(j, 0)
        for p in range(pairs):
            cols = pl.ds(p * KEYS, KEYS)
            e = expo[j, :, cols].astype(F32)
            d = (e * (prods[j, :, cols] * rows_of[0:1, cols] - rows_of[1:2, cols])).astype(BF16)
            ds[j, :, cols] = d
            dq = dot_t(keys, d)
            if j == 0:
                dq_t[:, cols] = dq
            else:
                dq_t[:, cols] += dq

    for j in range(NCH):
        if j == 0:
            second_pass(0)
        else:
            pl.when(has_back(j))(functools.partial(second_pass, j))

    for h in range(heads):
        cols = pl.ds(h * HD, HD)
        r = rq[h : h + 1, :]
        xn = qt[cols, :].astype(F32) * r
        gc = gain_t * (dq_t[:, cols] * (HD**-0.5))
        back = r * (gc - xn * jnp.mean(xn * gc, axis=0, keepdims=True))
        dqr_t[cols, :] = back.astype(BF16)

    loads[4].wait()

    def term(step, part):
        first = pl.multiple_of(head_at(step) * width + part * half, half)
        return dot(w_ref[pl.ds(first, half), :], dqr_t[...])

    def hand(slot, value, dst, recv, step):
        term_out[slot] = value.astype(BF16)
        return send(term_out.at[slot], dst, rs_send.at[slot], rs_recv.at[recv], (me, head_at(step)))

    mine = pl.ds(pl.multiple_of(core * BLOCK, BLOCK), BLOCK)
    theirs = pl.ds(pl.multiple_of(other * BLOCK, BLOCK), BLOCK)
    pt = [
        remote(part_out.at[j], part_in.at[j], pt_send.at[j], pt_recv.at[j], (sib, hx)) for j in range(NCH)
    ]
    cb = [None] + [
        remote(comb.at[j], arrived.at[j], cb_send.at[j], cb_recv.at[j], (ctx_at(-j), hx))
        for j in range(1, NCH)
    ]
    for j in range(NCH):
        always = None if j == 0 else has_back(j)
        sends.append((pt[j], always))
        if j > 0:
            sends.append((cb[j], always))

    def share(j):
        part_tmp[0] = dot_nt(qhat_t[...], ds[j])
        part_tmp[1] = dot_nt(gs_t[...], expo[j])
        for i in range(2):
            rows = slice(i * BLOCK, (i + 1) * BLOCK)
            part_own[j, rows, :] = part_tmp[i, :, mine]
            part_out[j, rows, :] = part_tmp[i, :, theirs].astype(BF16)
        pt[j].start()

    def pass_on(j):
        pt[j].wait_recv()
        summed = part_own[j] + part_in[j].astype(F32)
        if j > 0:
            comb[j] = summed.astype(BF16)
            cb[j].start()
        else:
            part_own[0] = summed

    def shares(chunks):
        for j in chunks:
            if j == 0:
                share(0)
            else:
                pl.when(has_back(j))(functools.partial(share, j))
            if j + 1 < NCH:
                pl.when(has_back(j + 1))(functools.partial(pass_on, j + 1))

    up_relay = hand(0, term(2, 0), relay_in.at[0], 0, 1)
    down_relay = hand(1, term(2, 1), relay_in.at[1], 1, -1)
    shares((5, 4, 3))
    direct_up = hand(2, term(1, 1), term_in.at[0, 1], 2, 1)
    direct_down = hand(3, term(-1, 0), term_in.at[1, 0], 3, -1)
    shares((2, 1, 0))
    part = term(1, 0)
    up_relay.wait_recv()
    summed_up = hand(4, part + relay_in[0].astype(F32), term_in.at[0, 0], 4, 1)
    part = term(-1, 1)
    down_relay.wait_recv()
    summed_down = hand(5, part + relay_in[1].astype(F32), term_in.at[1, 1], 5, -1)
    own = [term(0, 0), term(0, 1)]

    pass_on(0)
    for j in range(NCH - 1, 0, -1):

        @pl.when(has_next(j))
        def _():
            cb[j].wait_recv()
            part_own[0] += arrived[j].astype(F32)

    gv_ref[...] = part_own[0, BLOCK:, :].T.astype(BF16)
    k_f = k_ref[...].astype(F32)
    k_r = lax.rsqrt(jnp.mean(k_f * k_f, axis=-1, keepdims=True) + EPS)
    xn = k_f * k_r
    gc = kgain_ref[...] * (part_own[0, :BLOCK, :].T * (HD**-0.5))
    gk_ref[...] = (k_r * (gc - xn * jnp.mean(xn * gc, axis=-1, keepdims=True))).astype(BF16)

    for i, arrivals in enumerate(((summed_up, direct_down), (direct_up, summed_down))):
        for copy in arrivals:
            copy.wait_recv()
        sum_t = own[i] + term_in[0, i].astype(F32) + term_in[1, i].astype(F32)
        for b in range(half // BLOCK):
            first = i * half + b * BLOCK
            gi_ref[:, first : first + BLOCK] = sum_t[b * BLOCK : (b + 1) * BLOCK].T.astype(BF16)

    for copy, cond in sends:
        if cond is None:
            copy.wait_send()
        else:
            pl.when(cond)(copy.wait_send)


def hand_out(a, b, c, a_out, b_out, c_out, sem):
    copies = [
        pltpu.make_async_copy(src, dst, sem.at[i])
        for i, (src, dst) in enumerate(((a, a_out), (b, b_out), (c, c_out)))
    ]
    for copy in copies:
        copy.start()
    for copy in copies:
        copy.wait()


def local(mesh, *args):
    q, k, v, g, q_gain, k_gain, table, bucket, docs, w = args
    n_ctx, n_head = mesh.shape["ctx"], mesh.shape["head"]
    tokens, features = q.shape
    heads = features // HD
    cols = heads * BLOCK
    width = w.shape[0] // n_head
    half = width // 2
    vmem = pl.BlockSpec(memory_space=pltpu.VMEM)
    smem = pl.BlockSpec(memory_space=pltpu.SMEM)
    hbm = pl.BlockSpec(memory_space=pl.ANY)
    dma = pltpu.SemaphoreType.DMA
    results = pl.pallas_call(
        functools.partial(kernel, n_ctx, n_head, heads),
        out_shape=(
            pltpu.VMEM((tokens, width), BF16),
            pltpu.VMEM(k.shape, BF16),
            pltpu.VMEM(v.shape, BF16),
        ),
        in_specs=[vmem, smem, pl.BlockSpec(memory_space=pltpu.HBM), vmem, vmem, hbm, hbm, hbm, hbm, hbm],
        out_specs=(vmem, vmem, vmem),
        scratch_shapes=[
            pltpu.SMEM((1,), jnp.int32),
            pltpu.VMEM(q.shape, BF16),
            pltpu.VMEM(k.shape, BF16),
            pltpu.VMEM(v.shape, BF16),
            pltpu.VMEM(g.shape, BF16),
            pltpu.VMEM(w.shape, BF16),
            pltpu.VMEM((NCH, PAIR, KVROWS, HD), BF16),
            pltpu.VMEM((KEYS, BLOCK), F32),
            pltpu.VMEM((cols, BLOCK), BF16),
            pltpu.VMEM((heads, BLOCK), F32),
            pltpu.VMEM((HD, cols), BF16),
            pltpu.VMEM((HD, cols), BF16),
            pltpu.VMEM((HD, cols), BF16),
            pltpu.VMEM((8, cols), F32),
            pltpu.VMEM((8, cols), F32),
            pltpu.VMEM((HD, cols), F32),
            pltpu.VMEM((NCH, KEYS, cols), BF16),
            pltpu.VMEM((NCH, KEYS, cols), F32),
            pltpu.VMEM((NCH, KEYS, cols), BF16),
            pltpu.VMEM((HD, cols), F32),
            pltpu.VMEM((cols, BLOCK), BF16),
            pltpu.VMEM((2, HD, KEYS), F32),
            pltpu.VMEM((NCH, 2 * BLOCK, HD), F32),
            pltpu.VMEM((NCH, 2 * BLOCK, HD), BF16),
            pltpu.VMEM((NCH, 2 * BLOCK, HD), BF16),
            pltpu.VMEM((NCH, 2 * BLOCK, HD), BF16),
            pltpu.VMEM((NCH, 2 * BLOCK, HD), BF16),
            pltpu.VMEM((6, half, BLOCK), BF16),
            pltpu.VMEM((2, half, BLOCK), BF16),
            pltpu.VMEM((2, 2, half, BLOCK), BF16),
            dma((6,)),
            dma((NCH,)),
            dma((NCH,)),
            dma((NCH,)),
            dma((NCH,)),
            dma((NCH,)),
            dma((NCH,)),
            dma((NCH,)),
            dma((NCH,)),
            dma((6,)),
            dma((6,)),
        ],
        compiler_params=pltpu.CompilerParams(
            collective_id=0, has_side_effects=True, vmem_limit_bytes=56 * 1024 * 1024
        ),
    )(bucket.reshape(1, tokens), table, docs, q_gain.reshape(1, HD), k_gain.reshape(1, HD), q, k, v, g, w)
    return pl.pallas_call(
        hand_out,
        out_shape=tuple(jax.ShapeDtypeStruct(r.shape, r.dtype) for r in results),
        in_specs=[vmem] * 3,
        out_specs=(hbm,) * 3,
        scratch_shapes=[dma((3,))],
    )(*(pltpu.with_memory_space_constraint(r, pltpu.VMEM) for r in results))


def solution(mesh):
    placed = (
        P("ctx", "head"),
        P("ctx", "head"),
        P("ctx", "head"),
        P("ctx", "head"),
        P(),
        P(),
        P(),
        P("ctx"),
        P("ctx"),
        P(None, "head"),
    )
    return jax.shard_map(
        functools.partial(local, mesh),
        mesh=mesh,
        in_specs=placed,
        out_specs=(P("ctx", "head"), P("ctx", "head"), P("ctx", "head")),
        check_vma=False,
    )
```

time: 65.1 us -> 46 us (0.71)
  the two profiles are of different devices: /device:TPU:8 before, /device:TPU:24 now
where the time goes in v2:
time: 46 us; the launch traced here: 45.9 us
  Pallas kernels  44.6 us (97%)
  between operations  1.29 us (3%)
    pallas_call x1, Pallas kernels, local(): pl.pallas_call(functools.partial(kernel, n_ctx, n_head, heads), out_shape...  43.8 us

profile of v2, /device:TPU:24, one launch (start us, length us, event | category | flops | bytes accessed | tf_op | source)
XLA Modules:
  0.0 45.9 jit_solution(16929366831043402756)
XLA Ops:
  1.3 43.8 %shard_map.121 = (bf16[128,1024]{1,0:T(8,128)(2,1)S(1)}, bf16[128,128]{1,0:T(8,128)(2,1)S(1)}, bf16[128,128]{1,0:T(8,128)(2,1)S(1)}) custom-call(s32[1,128]{1,0:T(1,128)} %bitcast.3, f32[16]{0:T(128)} %table_ref.1, s32[1]{0:T(128)S(6)} %copy.13.doc_ref, f32[1,128]{1,0:T(1,128)} %bitcast.4, f32[1,128]{1,0:T(1,128)} %bitcast.5, bf16[128,1024]{1,0:T(8,128)(2,1)} %q_hbm.1, ...), custom_call_target="tpu_custom_call" | custom-call | tf_op jit(solution)/shard_map/pallas_call | solution.py:413
  45.1 0.7 %shard_map.122 = (bf16[128,1024]{1,0:T(8,128)(2,1)}, bf16[128,128]{1,0:T(8,128)(2,1)}, bf16[128,128]{1,0:T(8,128)(2,1)}) custom-call(bf16[128,1024]{1,0:T(8,128)(2,1)S(1)} %get-tuple-element.6.a, bf16[128,128]{1,0:T(8,128)(2,1)S(1)} %get-tuple-element.7.b, bf16[128,128]{1,0:T(8,128)(2,1)S(1)} %get-tuple-element.8.c), custom_call_target="tpu_custom_call" | custom-call | tf_op jit(solution)/shard_map/pallas_call | solution.py:469

commit v3 on v2

--- a/solution.py
+++ b/solution.py
@@ -39,11 +39,11 @@
     n_ctx,
     n_head,
     heads,
-    bucket_ref,
-    table_ref,
-    doc_ref,
-    qgain_ref,
-    kgain_ref,
+    bucket_hbm,
+    table_hbm,
+    doc_hbm,
+    qgain_hbm,
+    kgain_hbm,
     q_hbm,
     k_hbm,
     v_hbm,
@@ -52,7 +52,11 @@
     gi_ref,
     gk_ref,
     gv_ref,
-    doc_s,
+    bucket_ref,
+    table_ref,
+    doc_ref,
+    qgain_ref,
+    kgain_ref,
     q_ref,
     k_ref,
     v_ref,
@@ -82,6 +86,7 @@
     term_out,
     relay_in,
     term_in,
+    own,
     in_sem,
     kv_send,
     kv_recv,
@@ -100,7 +105,7 @@
     sib = me + 1 - 2 * core
     other = 1 - core
     width = gi_ref.shape[1]
-    half = width // 2
+    quarter = width // 4
     pairs = heads // 2
 
     chip = lax.div(me, PAIR)
@@ -117,17 +122,6 @@
 
     def head_at(step):
         return lax.rem(hx + step + n_head, n_head)
-
-    loads = [
-        pltpu.make_async_copy(k_hbm, k_ref, in_sem.at[0]),
-        pltpu.make_async_copy(v_hbm, v_ref, in_sem.at[1]),
-        pltpu.make_async_copy(q_hbm, q_ref, in_sem.at[2]),
-        pltpu.make_async_copy(g_hbm, g_ref, in_sem.at[3]),
-        pltpu.make_async_copy(w_hbm, w_ref, in_sem.at[4]),
-        pltpu.make_async_copy(doc_ref, doc_s, in_sem.at[5]),
-    ]
-    for i in (0, 1, 5, 2, 3, 4):
-        loads[i].start()
 
     barrier = pltpu.get_barrier_semaphore()
 
@@ -138,24 +132,39 @@
         greet(peer)
     for step in range(1, BACK + 1):
 
-        @pl.when(has_next(step))
-        def _():
-            greet((ctx_at(step), hx))
-
         @pl.when(has_back(step))
         def _():
             greet((ctx_at(-step), hx))
 
-    loads[5].wait()
-    own_doc = jnp.full((1, HD), doc_s[0], jnp.int32).astype(F32)
-    loads[0].wait()
-    loads[1].wait()
+    loads = [
+        pltpu.make_async_copy(src, dst, in_sem.at[i])
+        for i, (src, dst) in enumerate(
+            (
+                (k_hbm, k_ref),
+                (v_hbm, v_ref),
+                (kgain_hbm, kgain_ref),
+                (doc_hbm, doc_ref),
+                (q_hbm, q_ref),
+                (qgain_hbm, qgain_ref),
+                (table_hbm, table_ref),
+                (bucket_hbm, bucket_ref),
+                (g_hbm, g_ref),
+                (w_hbm, w_ref),
+            )
+        )
+    ]
+    for copy in loads:
+        copy.start()
+
+    for copy in loads[:4]:
+        copy.wait()
+    own_doc = jnp.full((1, HD), doc_ref[0], jnp.int32).astype(F32)
     k_f = k_ref[...].astype(F32)
     k_r = lax.rsqrt(jnp.mean(k_f * k_f, axis=-1, keepdims=True) + EPS)
     kvb[0, core, 0:BLOCK, :] = (k_f * k_r * kgain_ref[...]).astype(BF16)
     kvb[0, core, BLOCK : 2 * BLOCK, :] = v_ref[...]
     kvb[0, core, 2 * BLOCK : KVROWS, :] = jnp.broadcast_to(own_doc, (16, HD)).astype(BF16)
-    pl.semaphore_wait(barrier, 3 + jnp.minimum(chip, BACK) + jnp.minimum(chips - 1 - chip, BACK))
+    pl.semaphore_wait(barrier, 3 + jnp.minimum(chips - 1 - chip, BACK))
 
     sends = []
 
@@ -193,11 +202,12 @@
             send_if(has_next(j), own_kv, kvb.at[j, core], kv_send.at[j], kv_recv.at[j], (ctx_at(j), hx))
         )
 
+    for copy in loads[4:8]:
+        copy.wait()
     weight = jnp.zeros((1, BLOCK), F32)
     for b in range(NBUCKET):
         weight = jnp.where(bucket_ref[...] == b, table_ref[b], weight)
     gain_t = jnp.broadcast_to(qgain_ref[...], (HD, HD)).T
-    loads[2].wait()
     for h in range(heads):
         cols = pl.ds(h * HD, HD)
         x_t = q_ref[:, cols].T
@@ -206,7 +216,7 @@
         r = lax.rsqrt(jnp.mean(x * x, axis=0, keepdims=True) + EPS)
         rq[h : h + 1, :] = r
         qhat_t[:, cols] = (x * r * gain_t).astype(BF16)
-    loads[3].wait()
+    loads[8].wait()
     for h in range(heads):
         cols = pl.ds(h * HD, HD)
         g_t[:, cols] = g_ref[:, cols].T
@@ -291,15 +301,31 @@
         back = r * (gc - xn * jnp.mean(xn * gc, axis=0, keepdims=True))
         dqr_t[cols, :] = back.astype(BF16)
 
-    loads[4].wait()
+    loads[9].wait()
 
     def term(step, part):
-        first = pl.multiple_of(head_at(step) * width + part * half, half)
-        return dot(w_ref[pl.ds(first, half), :], dqr_t[...])
-
-    def hand(slot, value, dst, recv, step):
+        first = pl.multiple_of(head_at(step) * width + part * quarter, quarter)
+        return dot(w_ref[pl.ds(first, quarter), :], dqr_t[...])
+
+    def hand(slot, value, dst, step):
         term_out[slot] = value.astype(BF16)
-        return send(term_out.at[slot], dst, rs_send.at[slot], rs_recv.at[recv], (me, head_at(step)))
+        return send(term_out.at[slot], dst, rs_send.at[slot], rs_recv.at[slot], (me, head_at(step)))
+
+    def relay(side, q):
+        part = term(2, q + 2 * side)
+        return hand(side * 6 + q, part, relay_in.at[side, q], 1 - 2 * side)
+
+    def direct(side, q):
+        at = q + 2 - 2 * side
+        part = term(1 - 2 * side, at)
+        return hand(side * 6 + 2 + q, part, term_in.at[side, at], 1 - 2 * side)
+
+    def summed(side, q, arriving):
+        at = q + 2 * side
+        part = term(1 - 2 * side, at)
+        arriving.wait_recv()
+        part = part + relay_in[side, q].astype(F32)
+        return hand(side * 6 + 4 + q, part, term_in.at[side, at], 1 - 2 * side)
 
     mine = pl.ds(pl.multiple_of(core * BLOCK, BLOCK), BLOCK)
     theirs = pl.ds(pl.multiple_of(other * BLOCK, BLOCK), BLOCK)
@@ -343,19 +369,14 @@
             if j + 1 < NCH:
                 pl.when(has_back(j + 1))(functools.partial(pass_on, j + 1))
 
-    up_relay = hand(0, term(2, 0), relay_in.at[0], 0, 1)
-    down_relay = hand(1, term(2, 1), relay_in.at[1], 1, -1)
-    shares((5, 4, 3))
-    direct_up = hand(2, term(1, 1), term_in.at[0, 1], 2, 1)
-    direct_down = hand(3, term(-1, 0), term_in.at[1, 0], 3, -1)
-    shares((2, 1, 0))
-    part = term(1, 0)
-    up_relay.wait_recv()
-    summed_up = hand(4, part + relay_in[0].astype(F32), term_in.at[0, 0], 4, 1)
-    part = term(-1, 1)
-    down_relay.wait_recv()
-    summed_down = hand(5, part + relay_in[1].astype(F32), term_in.at[1, 1], 5, -1)
-    own = [term(0, 0), term(0, 1)]
+    relayed = {(side, q): relay(side, q) for q in range(2) for side in range(2)}
+    shares((5, 4))
+    straight = {(side, q): direct(side, q) for q in range(2) for side in range(2)}
+    shares((3, 2))
+    added = {(side, q): summed(side, q, relayed[side, q]) for q in range(2) for side in range(2)}
+    shares((1, 0))
+    for q in range(4):
+        own[q] = term(0, q)
 
     pass_on(0)
     for j in range(NCH - 1, 0, -1):
@@ -372,13 +393,18 @@
     gc = kgain_ref[...] * (part_own[0, :BLOCK, :].T * (HD**-0.5))
     gk_ref[...] = (k_r * (gc - xn * jnp.mean(xn * gc, axis=-1, keepdims=True))).astype(BF16)
 
-    for i, arrivals in enumerate(((summed_up, direct_down), (direct_up, summed_down))):
+    for q, arrivals in (
+        (0, (added[0, 0], straight[1, 0])),
+        (2, (straight[0, 0], added[1, 0])),
+        (1, (added[0, 1], straight[1, 1])),
+        (3, (straight[0, 1], added[1, 1])),
+    ):
         for copy in arrivals:
             copy.wait_recv()
-        sum_t = own[i] + term_in[0, i].astype(F32) + term_in[1, i].astype(F32)
-        for b in range(half // BLOCK):
-            first = i * half + b * BLOCK
-            gi_ref[:, first : first + BLOCK] = sum_t[b * BLOCK : (b + 1) * BLOCK].T.astype(BF16)
+        sum_t = (own[q] + term_in[0, q].astype(F32) + term_in[1, q].astype(F32)).astype(BF16)
+        for b in range(quarter // BLOCK):
+            first = q * quarter + b * BLOCK
+            gi_ref[:, first : first + BLOCK] = sum_t[b * BLOCK : (b + 1) * BLOCK].T
 
     for copy, cond in sends:
         if cond is None:
@@ -405,7 +431,7 @@
     heads = features // HD
     cols = heads * BLOCK
     width = w.shape[0] // n_head
-    half = width // 2
+    quarter = width // 4
     vmem = pl.BlockSpec(memory_space=pltpu.VMEM)
     smem = pl.BlockSpec(memory_space=pltpu.SMEM)
     hbm = pl.BlockSpec(memory_space=pl.ANY)
@@ -417,10 +443,14 @@
             pltpu.VMEM(k.shape, BF16),
             pltpu.VMEM(v.shape, BF16),
         ),
-        in_specs=[vmem, smem, pl.BlockSpec(memory_space=pltpu.HBM), vmem, vmem, hbm, hbm, hbm, hbm, hbm],
+        in_specs=[hbm, pl.BlockSpec(memory_space=pltpu.HBM), pl.BlockSpec(memory_space=pltpu.HBM)] + [hbm] * 7,
         out_specs=(vmem, vmem, vmem),
         scratch_shapes=[
+            pltpu.VMEM((1, tokens), jnp.int32),
+            pltpu.SMEM((NBUCKET,), F32),
             pltpu.SMEM((1,), jnp.int32),
+            pltpu.VMEM((1, HD), F32),
+            pltpu.VMEM((1, HD), F32),
             pltpu.VMEM(q.shape, BF16),
             pltpu.VMEM(k.shape, BF16),
             pltpu.VMEM(v.shape, BF16),
@@ -447,20 +477,21 @@
             pltpu.VMEM((NCH, 2 * BLOCK, HD), BF16),
             pltpu.VMEM((NCH, 2 * BLOCK, HD), BF16),
             pltpu.VMEM((NCH, 2 * BLOCK, HD), BF16),
-            pltpu.VMEM((6, half, BLOCK), BF16),
-            pltpu.VMEM((2, half, BLOCK), BF16),
-            pltpu.VMEM((2, 2, half, BLOCK), BF16),
-            dma((6,)),
-            dma((NCH,)),
-            dma((NCH,)),
-            dma((NCH,)),
-            dma((NCH,)),
-            dma((NCH,)),
-            dma((NCH,)),
-            dma((NCH,)),
-            dma((NCH,)),
-            dma((6,)),
-            dma((6,)),
+            pltpu.VMEM((12, quarter, BLOCK), BF16),
+            pltpu.VMEM((2, 2, quarter, BLOCK), BF16),
+            pltpu.VMEM((2, 4, quarter, BLOCK), BF16),
+            pltpu.VMEM((4, quarter, BLOCK), F32),
+            dma((10,)),
+            dma((NCH,)),
+            dma((NCH,)),
+            dma((NCH,)),
+            dma((NCH,)),
+            dma((NCH,)),
+            dma((NCH,)),
+            dma((NCH,)),
+            dma((NCH,)),
+            dma((12,)),
+            dma((12,)),
         ],
         compiler_params=pltpu.CompilerParams(
             collective_id=0, has_side_effects=True, vmem_limit_bytes=56 * 1024 * 1024

time: 46 us -> 40.1 us (0.87)
  the two profiles are of different devices: /device:TPU:24 before, /device:TPU:249 now
where the time goes in v3:
time: 40.1 us; the launch traced here: 40 us
  Pallas kernels  38.7 us (97%)
  between operations  1.29 us (3%)
    pallas_call x1, Pallas kernels, local(): pl.pallas_call(functools.partial(kernel, n_ctx, n_head, heads), out_shape...  37.9 us

profile of v3, /device:TPU:249, one launch (start us, length us, event | category | flops | bytes accessed | tf_op | source)
XLA Modules:
  0.0 40.0 jit_solution(6350149255769871501)
XLA Ops:
  1.3 37.9 %shard_map.121 = (bf16[128,1024]{1,0:T(8,128)(2,1)S(1)}, bf16[128,128]{1,0:T(8,128)(2,1)S(1)}, bf16[128,128]{1,0:T(8,128)(2,1)S(1)}) custom-call(s32[1,128]{1,0:T(1,128)} %bitcast.3, f32[16]{0:T(128)} %table_hbm.1, s32[1]{0:T(128)S(6)} %copy.13.doc_hbm, f32[1,128]{1,0:T(1,128)} %bitcast.4, f32[1,128]{1,0:T(1,128)} %bitcast.5, bf16[128,1024]{1,0:T(8,128)(2,1)} %q_hbm.1, ...), custom_call_target="tpu_custom_call" | custom-call | tf_op jit(solution)/shard_map/pallas_call | solution.py:439
  39.2 0.7 %shard_map.122 = (bf16[128,1024]{1,0:T(8,128)(2,1)}, bf16[128,128]{1,0:T(8,128)(2,1)}, bf16[128,128]{1,0:T(8,128)(2,1)}) custom-call(bf16[128,1024]{1,0:T(8,128)(2,1)S(1)} %get-tuple-element.6.a, bf16[128,128]{1,0:T(8,128)(2,1)S(1)} %get-tuple-element.7.b, bf16[128,128]{1,0:T(8,128)(2,1)S(1)} %get-tuple-element.8.c), custom_call_target="tpu_custom_call" | custom-call | tf_op jit(solution)/shard_map/pallas_call | solution.py:500

commit v4 on v3

--- a/solution.py
+++ b/solution.py
@@ -14,6 +14,8 @@
 PAIR = 2
 BACK = HOPS // PAIR
 NCH = BACK + 1
+ROW = 4
+ORDER = (0, 4, 1, 2, 3, 5)
 KEYS = PAIR * BLOCK
 KVROWS = 2 * BLOCK + 16
 EPS = 1e-06
@@ -90,6 +92,7 @@
     in_sem,
     kv_send,
     kv_recv,
+    rl_send,
     fw_send,
     fw_recv,
     pt_send,
@@ -110,6 +113,7 @@
 
     chip = lax.div(me, PAIR)
     chips = n_ctx // PAIR
+    place = lax.rem(chip, ROW)
 
     def has_back(step):
         return chip >= step
@@ -130,11 +134,19 @@
 
     for peer in [(sib, hx), (me, head_at(1)), (me, head_at(-1))]:
         greet(peer)
-    for step in range(1, BACK + 1):
-
-        @pl.when(has_back(step))
-        def _():
-            greet((ctx_at(-step), hx))
+    for step in range(1, ROW):
+        greet((ctx_at(lax.rem(place + step, ROW) - place), hx))
+
+    @pl.when(has_back(ROW))
+    def _():
+        greet((ctx_at(-ROW), hx))
+
+    starts_row = place == 0
+    ends_row = place == ROW - 1
+
+    @pl.when(jnp.logical_and(starts_row, has_back(1)))
+    def _():
+        greet((ctx_at(-1), hx))
 
     loads = [
         pltpu.make_async_copy(src, dst, in_sem.at[i])
@@ -164,7 +176,8 @@
     kvb[0, core, 0:BLOCK, :] = (k_f * k_r * kgain_ref[...]).astype(BF16)
     kvb[0, core, BLOCK : 2 * BLOCK, :] = v_ref[...]
     kvb[0, core, 2 * BLOCK : KVROWS, :] = jnp.broadcast_to(own_doc, (16, HD)).astype(BF16)
-    pl.semaphore_wait(barrier, 3 + jnp.minimum(chips - 1 - chip, BACK))
+    awaited = 3 + ROW - 1 + jnp.where(has_next(ROW), 1, 0) + jnp.where(jnp.logical_and(ends_row, has_next(1)), 1, 0)
+    pl.semaphore_wait(barrier, awaited)
 
     sends = []
 
@@ -196,11 +209,31 @@
         slot = kvb.at[j, core]
         fw.append(remote(slot, slot, fw_send.at[j], fw_recv.at[j], (sib, hx)))
         sends.append((fw[j], has_back(j)))
+    for step in range(1, ROW):
+        send_if(
+            place + step < ROW, own_kv, kvb.at[step, core], kv_send.at[step], kv_recv.at[step], (ctx_at(step), hx)
+        )
+    send_if(
+        has_next(ROW), own_kv, kvb.at[ROW, core], kv_send.at[ROW], kv_recv.at[ROW], (ctx_at(ROW), hx)
+    )
     kv = [None]
     for j in range(1, NCH):
-        kv.append(
-            send_if(has_next(j), own_kv, kvb.at[j, core], kv_send.at[j], kv_recv.at[j], (ctx_at(j), hx))
+        slot = kvb.at[j, core]
+        kv.append(remote(slot, slot, kv_send.at[j], kv_recv.at[j], (sib, hx)))
+    relays = []
+    for i, (step, cond) in enumerate(
+        ((1, has_next(1)), (-1, place >= 1), (-2, place >= 2), (-3, place >= 3))
+    ):
+        far = ROW + step
+        relays.append(
+            (
+                cond,
+                remote(
+                    kvb.at[ROW, core], kvb.at[far, core], rl_send.at[i], kv_recv.at[far], (ctx_at(step), hx)
+                ),
+            )
         )
+        sends.append((relays[i][1], jnp.logical_and(cond, has_back(ROW))))
 
     for copy in loads[4:8]:
         copy.wait()
@@ -228,10 +261,16 @@
     def both(j, first):
         return jnp.concatenate([kvb[j, b, first : first + BLOCK, :] for b in range(PAIR)], axis=0)
 
-    def first_pass(j):
-        if j > 0:
+    def fetch(j):
+        @pl.when(has_back(j))
+        def _():
             kv[j].wait_recv()
+            if j == ROW:
+                for cond, copy in relays:
+                    pl.when(cond)(copy.start)
             fw[j].start()
+
+    def first_pass(j, following):
         fw[j].wait_recv()
         for b in range(PAIR):
             docs = kvb[j, b, 2 * BLOCK : KVROWS, :].astype(F32)[0:1]
@@ -258,12 +297,16 @@
             else:
                 total[:, cols] += part
                 out_t[:, cols] += weighted
-
-    for j in range(NCH):
+            if p == 0 and following is not None:
+                fetch(following)
+
+    for j, following in zip(ORDER, ORDER[1:] + (None,)):
         if j == 0:
-            first_pass(0)
+            first_pass(0, following)
         else:
-            pl.when(has_back(j))(functools.partial(first_pass, j))
+            pl.when(has_back(j))(functools.partial(first_pass, j, following))
+            if following is not None:
+                pl.when(jnp.logical_not(has_back(j)))(functools.partial(fetch, following))
 
     for p in range(pairs):
         cols = pl.ds(p * KEYS, KEYS)
@@ -484,6 +527,7 @@
             dma((10,)),
             dma((NCH,)),
             dma((NCH,)),
+            dma((4,)),
             dma((NCH,)),
             dma((NCH,)),
             dma((NCH,)),

time: 40.1 us -> 44.9 us (1.12)
  the two profiles are of different devices: /device:TPU:249 before, /device:TPU:24 now
where the time goes in v4:
time: 44.9 us; the launch traced here: 44.7 us
  Pallas kernels  43.4 us (97%)
  between operations  1.29 us (3%)
    pallas_call x1, Pallas kernels, local(): pl.pallas_call(functools.partial(kernel, n_ctx, n_head, heads), out_shape...  42.7 us

profile of v4, /device:TPU:24, one launch (start us, length us, event | category | flops | bytes accessed | tf_op | source)
XLA Modules:
  0.0 44.7 jit_solution(314787945705155620)
XLA Ops:
  1.3 42.7 %shard_map.121 = (bf16[128,1024]{1,0:T(8,128)(2,1)S(1)}, bf16[128,128]{1,0:T(8,128)(2,1)S(1)}, bf16[128,128]{1,0:T(8,128)(2,1)S(1)}) custom-call(s32[1,128]{1,0:T(1,128)} %bitcast.3, f32[16]{0:T(128)} %table_hbm.1, s32[1]{0:T(128)S(6)} %copy.13.doc_hbm, f32[1,128]{1,0:T(1,128)} %bitcast.4, f32[1,128]{1,0:T(1,128)} %bitcast.5, bf16[128,1024]{1,0:T(8,128)(2,1)} %q_hbm.1, ...), custom_call_target="tpu_custom_call" | custom-call | tf_op jit(solution)/shard_map/pallas_call | solution.py:482
  44.0 0.7 %shard_map.122 = (bf16[128,1024]{1,0:T(8,128)(2,1)}, bf16[128,128]{1,0:T(8,128)(2,1)}, bf16[128,128]{1,0:T(8,128)(2,1)}) custom-call(bf16[128,1024]{1,0:T(8,128)(2,1)S(1)} %get-tuple-element.6.a, bf16[128,128]{1,0:T(8,128)(2,1)S(1)} %get-tuple-element.7.b, bf16[128,128]{1,0:T(8,128)(2,1)S(1)} %get-tuple-element.8.c), custom_call_target="tpu_custom_call" | custom-call | tf_op jit(solution)/shard_map/pallas_call | solution.py:544

commit v5 on v3

--- a/solution.py
+++ b/solution.py
@@ -228,10 +228,13 @@
     def both(j, first):
         return jnp.concatenate([kvb[j, b, first : first + BLOCK, :] for b in range(PAIR)], axis=0)
 
-    def first_pass(j):
-        if j > 0:
+    def fetch(j):
+        @pl.when(has_back(j))
+        def _():
             kv[j].wait_recv()
             fw[j].start()
+
+    def first_pass(j):
         fw[j].wait_recv()
         for b in range(PAIR):
             docs = kvb[j, b, 2 * BLOCK : KVROWS, :].astype(F32)[0:1]
@@ -258,6 +261,8 @@
             else:
                 total[:, cols] += part
                 out_t[:, cols] += weighted
+            if p == pairs - 2 and j + 1 < NCH:
+                fetch(j + 1)
 
     for j in range(NCH):
         if j == 0:
@@ -362,19 +367,18 @@
 
     def shares(chunks):
         for j in chunks:
-            if j == 0:
-                share(0)
-            else:
-                pl.when(has_back(j))(functools.partial(share, j))
+            pl.when(has_back(j))(functools.partial(share, j))
             if j + 1 < NCH:
                 pl.when(has_back(j + 1))(functools.partial(pass_on, j + 1))
 
     relayed = {(side, q): relay(side, q) for q in range(2) for side in range(2)}
     shares((5, 4))
     straight = {(side, q): direct(side, q) for q in range(2) for side in range(2)}
-    shares((3, 2))
-    added = {(side, q): summed(side, q, relayed[side, q]) for q in range(2) for side in range(2)}
-    shares((1, 0))
+    shares((3, 2, 1))
+    added = {(side, 0): summed(side, 0, relayed[side, 0]) for side in range(2)}
+    pl.when(has_back(1))(functools.partial(pass_on, 1))
+    added |= {(side, 1): summed(side, 1, relayed[side, 1]) for side in range(2)}
+    share(0)
     for q in range(4):
         own[q] = term(0, q)
 

time: 40.1 us -> 39.8 us (level)
  the two profiles are of different devices: /device:TPU:249 before, /device:TPU:120 now
where the time goes in v5:
time: 39.8 us; the launch traced here: 39.6 us
  Pallas kernels  38.4 us (96%)
  between operations  1.29 us (3%)
    pallas_call x1, Pallas kernels, local(): pl.pallas_call(functools.partial(kernel, n_ctx, n_head, heads), out_shape...  37.6 us

profile of v5, /device:TPU:120, one launch (start us, length us, event | category | flops | bytes accessed | tf_op | source)
XLA Modules:
  0.0 39.6 jit_solution(3320180441272549196)
XLA Ops:
  1.3 37.6 %shard_map.121 = (bf16[128,1024]{1,0:T(8,128)(2,1)S(1)}, bf16[128,128]{1,0:T(8,128)(2,1)S(1)}, bf16[128,128]{1,0:T(8,128)(2,1)S(1)}) custom-call(s32[1,128]{1,0:T(1,128)} %bitcast.3, f32[16]{0:T(128)} %table_hbm.1, s32[1]{0:T(128)S(6)} %copy.13.doc_hbm, f32[1,128]{1,0:T(1,128)} %bitcast.4, f32[1,128]{1,0:T(1,128)} %bitcast.5, bf16[128,1024]{1,0:T(8,128)(2,1)} %q_hbm.1, ...), custom_call_target="tpu_custom_call" | custom-call | tf_op jit(solution)/shard_map/pallas_call | solution.py:443
  38.9 0.7 %shard_map.122 = (bf16[128,1024]{1,0:T(8,128)(2,1)}, bf16[128,128]{1,0:T(8,128)(2,1)}, bf16[128,128]{1,0:T(8,128)(2,1)}) custom-call(bf16[128,1024]{1,0:T(8,128)(2,1)S(1)} %get-tuple-element.6.a, bf16[128,128]{1,0:T(8,128)(2,1)S(1)} %get-tuple-element.7.b, bf16[128,128]{1,0:T(8,128)(2,1)S(1)} %get-tuple-element.8.c), custom_call_target="tpu_custom_call" | custom-call | tf_op jit(solution)/shard_map/pallas_call | solution.py:504

commit v6 on v5

--- a/solution.py
+++ b/solution.py
@@ -15,7 +15,7 @@
 BACK = HOPS // PAIR
 NCH = BACK + 1
 KEYS = PAIR * BLOCK
-KVROWS = 2 * BLOCK + 16
+KVROWS = 2 * BLOCK + 8
 EPS = 1e-06
 MESH = pl.DeviceIdType.MESH
 F32 = jnp.float32
@@ -163,7 +163,7 @@
     k_r = lax.rsqrt(jnp.mean(k_f * k_f, axis=-1, keepdims=True) + EPS)
     kvb[0, core, 0:BLOCK, :] = (k_f * k_r * kgain_ref[...]).astype(BF16)
     kvb[0, core, BLOCK : 2 * BLOCK, :] = v_ref[...]
-    kvb[0, core, 2 * BLOCK : KVROWS, :] = jnp.broadcast_to(own_doc, (16, HD)).astype(BF16)
+    kvb[0, core, 2 * BLOCK : KVROWS, :] = jnp.broadcast_to(own_doc, (8, HD)).astype(BF16)
     pl.semaphore_wait(barrier, 3 + jnp.minimum(chips - 1 - chip, BACK))
 
     sends = []
@@ -261,7 +261,7 @@
             else:
                 total[:, cols] += part
                 out_t[:, cols] += weighted
-            if p == pairs - 2 and j + 1 < NCH:
+            if p == 1 and j + 1 < NCH:
                 fetch(j + 1)
 
     for j in range(NCH):

time: 39.8 us -> 39 us (0.980)
  the two profiles are of different devices: /device:TPU:120 before, /device:TPU:248 now
where the time goes in v6:
time: 39 us; the launch traced here: 38.8 us
  Pallas kernels  37.5 us (96%)
  between operations  1.29 us (3%)
    pallas_call x1, Pallas kernels, local(): pl.pallas_call(functools.partial(kernel, n_ctx, n_head, heads), out_shape...  36.8 us

profile of v6, /device:TPU:248, one launch (start us, length us, event | category | flops | bytes accessed | tf_op | source)
XLA Modules:
  0.0 38.8 jit_solution(9252634848897384765)
XLA Ops:
  1.3 36.8 %shard_map.121 = (bf16[128,1024]{1,0:T(8,128)(2,1)S(1)}, bf16[128,128]{1,0:T(8,128)(2,1)S(1)}, bf16[128,128]{1,0:T(8,128)(2,1)S(1)}) custom-call(s32[1,128]{1,0:T(1,128)} %bitcast.3, f32[16]{0:T(128)} %table_hbm.1, s32[1]{0:T(128)S(6)} %copy.13.doc_hbm, f32[1,128]{1,0:T(1,128)} %bitcast.4, f32[1,128]{1,0:T(1,128)} %bitcast.5, bf16[128,1024]{1,0:T(8,128)(2,1)} %q_hbm.1, ...), custom_call_target="tpu_custom_call" | custom-call | tf_op jit(solution)/shard_map/pallas_call | solution.py:443
  38.1 0.7 %shard_map.122 = (bf16[128,1024]{1,0:T(8,128)(2,1)}, bf16[128,128]{1,0:T(8,128)(2,1)}, bf16[128,128]{1,0:T(8,128)(2,1)}) custom-call(bf16[128,1024]{1,0:T(8,128)(2,1)S(1)} %get-tuple-element.6.a, bf16[128,128]{1,0:T(8,128)(2,1)S(1)} %get-tuple-element.7.b, bf16[128,128]{1,0:T(8,128)(2,1)S(1)} %get-tuple-element.8.c), custom_call_target="tpu_custom_call" | custom-call | tf_op jit(solution)/shard_map/pallas_call | solution.py:504
